TPU v7x, 32 devices: a whole 2x2x4 slice. The times are simulated.
32 devices in a mesh: dp: 8 (over z, core), ctx: 4 (over y, x).
Axes of the slice: x: 2, y: 2, z: 4, core: 2. Of those that a mesh axis runs over, the one named last changes fastest.
Arguments:
- layer_input: bfloat16 [8, 640, 4096], P('dp', 'ctx'), may hold values from -6 to 6
- queries: bfloat16 [8, 640, 2048], P('dp', 'ctx'), may hold values from -6 to 6, as said below
- key_rows: bfloat16 [8, 640, 2048], P('dp', 'ctx'), may hold values from -6 to 6, as said below
- value_rows: bfloat16 [8, 640, 2048], P('dp', 'ctx'), may hold values from -6 to 6
- attn_out: bfloat16 [8, 640, 2048], P('dp', 'ctx'), may hold values from -3 to 3
- out_grad: bfloat16 [8, 640, 2048], P('dp', 'ctx'), may hold values from -0.15625 to 0.15625
- layer_grad: bfloat16 [8, 640, 4096], P('dp', 'ctx'), may hold values from -0.078125 to 0.078125
- logsum: float32 [8, 16, 640], P('dp'), may hold values from -12 to 16, as said below
- projector: bfloat16 [4096, 512], replicated, may hold values from -0.09375 to 0.09375
Outputs:
- weight_grads: float32 [4, 512, 2048], P(None, ('dp', 'ctx'))
Inputs may be any that keep to these rules, and one draw needn't show every extreme that they name: `queries`: drawn together with key_rows and logsum. `key_rows`: drawn together with queries and logsum.
All inputs are finite; a program needn't handle non-finite values.
Results may differ from a plain program's by a relative error of at most 0.0033.
Values may be sent and summed in bfloat16 or wider, within the bound.
A program may use at most 320 MiB of HBM per device.

v0:
```python
import math

import jax
import jax.numpy as jnp
from jax import lax
from jax.sharding import PartitionSpec as P


def contract_rows(left, right):
    return lax.dot_general(
        left, right, (((0,), (0,)), ((), ())), preferred_element_type=jnp.float32
    )


def project_split(reduced, values):
    upper_part = values.astype(jnp.bfloat16)
    remainder = (values - upper_part.astype(jnp.float32)).astype(jnp.bfloat16)
    return contract_rows(reduced, upper_part) + contract_rows(reduced, remainder)


def query_grads(
    query_part,
    grad_part,
    deltas,
    sums_part,
    query_start,
    piece_keys,
    piece_values,
    scaling,
    head_count,
):
    row_count = query_part.shape[0]
    key_count = piece_keys.shape[0]
    feature_width = query_part.shape[1]
    head_dim = feature_width // head_count
    query3 = query_part.reshape(row_count, head_count, head_dim)
    grad3 = grad_part.reshape(row_count, head_count, head_dim)
    key3 = piece_keys.reshape(key_count, head_count, head_dim)
    value3 = piece_values.reshape(key_count, head_count, head_dim)
    scores = jnp.einsum("thd,uhd->htu", query3, key3, preferred_element_type=jnp.float32) * scaling
    query_pos = query_start + lax.iota(jnp.int32, row_count)
    key_pos = lax.iota(jnp.int32, key_count)
    causal = query_pos[:, None] >= key_pos[None, :]
    prob = jnp.where(causal[None], jnp.exp(scores - sums_part[:, :, None]), jnp.float32(0.0))
    dprob = jnp.einsum("thd,uhd->htu", grad3, value3, preferred_element_type=jnp.float32)
    dscore = prob * (dprob - deltas[:, :, None]) * scaling
    score_low = dscore.astype(jnp.bfloat16)
    prob_low = prob.astype(jnp.bfloat16)
    dquery = jnp.einsum(
        "htu,uhd->thd", score_low, key3, preferred_element_type=jnp.float32
    ).reshape(row_count, feature_width)
    dkey = jnp.einsum(
        "htu,thd->uhd", score_low, query3, preferred_element_type=jnp.float32
    ).reshape(key_count, feature_width)
    dvalue = jnp.einsum(
        "htu,thd->uhd", prob_low, grad3, preferred_element_type=jnp.float32
    ).reshape(key_count, feature_width)
    return (dquery, dkey, dvalue)


def on_device(
    layer_input, queries, key_rows, value_rows, attn_out, out_grad, layer_grad, logsum, projector
):
    own_queries = queries[0]
    own_keys = key_rows[0]
    own_values = value_rows[0]
    own_out = attn_out[0]
    own_grad = out_grad[0]
    sums_all = logsum[0]
    head_count = sums_all.shape[0]
    tokens = own_queries.shape[0]
    half_rows = tokens // 2
    feature_width = own_queries.shape[1]
    rank_width = projector.shape[1]
    scaling = 1.0 / math.sqrt(feature_width // head_count)
    ctx_index = lax.axis_index("ctx")
    reduced_in = jnp.dot(layer_input[0], projector, preferred_element_type=jnp.float32).astype(
        jnp.bfloat16
    )
    reduced_grad = jnp.dot(layer_grad[0], projector, preferred_element_type=jnp.float32).astype(
        jnp.bfloat16
    )
    grad_output = contract_rows(reduced_grad, own_out)
    lower_rows = (
        own_queries[:half_rows],
        own_grad[:half_rows],
        own_out[:half_rows],
        reduced_in[:half_rows],
    )
    upper_rows = (
        own_queries[half_rows:],
        own_grad[half_rows:],
        own_out[half_rows:],
        reduced_in[half_rows:],
    )
    lower_start = ctx_index * tokens
    upper_start = ctx_index * tokens + half_rows
    groups = []
    for members, first_row in ((lower_rows, lower_start), (upper_rows, upper_start)):
        query_part, grad_part, out_part, reduced_part = members
        deltas = (
            (grad_part.astype(jnp.float32) * out_part.astype(jnp.float32))
            .reshape(half_rows, head_count, -1)
            .sum(axis=-1)
            .T
        )
        sums_part = lax.dynamic_slice_in_dim(sums_all, first_row, half_rows, 1)
        groups.append((query_part, grad_part, deltas, sums_part, first_row, reduced_part))
    last_position = jnp.maximum(lower_start, upper_start) + half_rows - 1
    offset = jnp.int32(0)
    grad_key = jnp.zeros((rank_width, feature_width), jnp.float32)
    grad_value = jnp.zeros((rank_width, feature_width), jnp.float32)
    piece_keys = lax.all_gather(own_keys, "ctx", axis=0, tiled=True)
    piece_values = lax.all_gather(own_values, "ctx", axis=0, tiled=True)
    piece_reduced = lax.all_gather(reduced_in, "ctx", axis=0, tiled=True)
    key_count = piece_keys.shape[0]

    def one_group(member):
        query_part, grad_part, deltas, sums_part, query_start, unused = member

        def active():
            return query_grads(
                query_part,
                grad_part,
                deltas,
                sums_part,
                query_start,
                piece_keys,
                piece_values,
                scaling,
                head_count,
            )

        def skipped():
            zero_query = jnp.zeros((half_rows, feature_width), jnp.float32)
            zero_key = jnp.zeros((key_count, feature_width), jnp.float32)
            return (zero_query, zero_key, zero_key)

        return lax.cond(offset <= query_start + half_rows - 1, active, skipped)

    lower_out = one_group(groups[0])
    upper_out = one_group(groups[1])

    def project():
        joined = jnp.concatenate([lower_out[1] + upper_out[1], lower_out[2] + upper_out[2]], axis=1)
        both = project_split(piece_reduced, joined)
        return (both[:, :feature_width], both[:, feature_width:])

    def unchanged():
        return (grad_key, grad_value)

    grad_key, grad_value = lax.cond(offset <= last_position, project, unchanged)
    grad_query = project_split(groups[0][5], lower_out[0]) + project_split(
        groups[1][5], upper_out[0]
    )
    stacked = jnp.stack([grad_query, grad_key, grad_value, grad_output])
    summed = lax.psum_scatter(stacked, "dp", scatter_dimension=1, tiled=True)
    summed = lax.psum_scatter(summed, "ctx", scatter_dimension=1, tiled=True)
    return summed


def solution(mesh):
    placed = (
        P("dp", "ctx", None),
        P("dp", "ctx", None),
        P("dp", "ctx", None),
        P("dp", "ctx", None),
        P("dp", "ctx", None),
        P("dp", "ctx", None),
        P("dp", "ctx", None),
        P("dp", None, None),
        P(),
    )
    return jax.shard_map(
        on_device,
        mesh=mesh,
        in_specs=placed,
        out_specs=P(None, ("dp", "ctx"), None),
        check_vma=False,
    )
```

profile of v0, /device:TPU:0, one launch (start us, length us, event | category | flops | bytes accessed | tf_op | source)
XLA Modules:
  0.0 439.9 jit_solution(1880834849122164969)
XLA Ops:
  6.5 0.7 all-gather.5.cloned.1.call-update
  7.3 0.7 all-gather.7.cloned.1.call-update
  8.1 1.4 multiply_bitcast_fusion
  9.5 0.1 copy.86
  9.6 0.1 copy.87
  9.8 0.2 reduce_sum.18
  10.0 0.2 reduce_sum.19
  10.3 3.5 fusion.65
  13.8 17.7 %all_gather.11 = bf16[640,512]{1,0:T(8,128)(2,1)} all-gather(bf16[160,512]{1,0:T(8,128)(2,1)S(1)} %fusion.65), channel_id=1, replica_groups=mesh['dp'=8,'ctx'=4] {'ctx'}, dimensions={0}, use_global_device_ids=true | all-gather | bytes 819200 | tf_op jit(solution)/shard_map/all_gather | solution.py:115
  31.5 5.8 %convolution_bitcast_fusion = f32[1,512,2048]{2,1,0:T(8,128)} fusion(bf16[1,160,2048]{2,1,0:T(8,128)(2,1)S(1)} %copy-done.8, bf16[4096,512]{1,0:T(8,128)(2,1)} %param.23, bf16[1,160,4096]{2,1,0:T(8,128)(2,1)S(1)} %copy-done), kind=kOutput, calls=%fused_computation.71 | convolution fusion | flops 1006714880 | bytes 10354688 | tf_op jit(solution)/shard_map/dot_general | solution.py:10
  37.4 17.6 %all-gather.5.cloned.1.call-done = bf16[1,640,2048]{2,1,0:T(8,128)(2,1)} async-done(((bf16[1,160,2048]{2,1,0:T(8,128)(2,1)}), bf16[1,640,2048]{2,1,0:T(8,128)(2,1)}) %all-gather.5.cloned.1.call-update) | async-done | bytes 2621456 | tf_op jit(solution)/shard_map/all_gather | solution.py:113
  55.0 41.4 %all-gather.7.cloned.1.call-done = bf16[1,640,2048]{2,1,0:T(8,128)(2,1)} async-done(((bf16[1,160,2048]{2,1,0:T(8,128)(2,1)}), bf16[1,640,2048]{2,1,0:T(8,128)(2,1)}) %all-gather.7.cloned.1.call-update) | async-done | bytes 2621456 | tf_op jit(solution)/shard_map/all_gather | solution.py:114
  96.3 20.1 %conditional.3 = (f32[80,2048]{1,0:T(8,128)S(1)}, f32[640,2048]{0,1:T(8,128)}, f32[640,2048]{0,1:T(8,128)}, bf16[80,2048]{1,0:T(8,128)(2,1)S(1)}) conditional(s32[]{:T(128)} %convert_element_type.103, () %tuple.43, (s32[]{:T(128)}, bf16[1,160,2048]{2,1,0:T(8,128)(2,1)}, bf16[640,2048]{1,0:T(8,128)(2,1)}, f32[1,16,640]{2,1,0:T(8,128)}, ...), branch_computations={%region_1.0_spmd, %region_2.0_spmd} | conditional | flops 1057802304 | bytes 62449412 | solution.py:139
  96.3 0.8 dynamic-slice_bitcast_fusion
  97.2 1.0 slice_bitcast_fusion
  98.3 4.7 %fusion.5 = f32[16,80,640]{2,1,0:T(8,128)} fusion(bf16[80,16,128]{2,1,0:T(8,128)(2,1)S(1)} %bitcast.141, bf16[640,2048]{1,0:T(8,128)(2,1)} %get-tuple-element.122), kind=kOutput, calls=%fused_computation.7 | convolution fusion | flops 209715200 | bytes 6225920 | tf_op jit(solution)/shard_map/cond/branch_1_fun/thd,uhd->htu/dot_general | solution.py:40
  103.1 5.9 %multiply_convert_fusion = bf16[16,80,640]{2,1,0:T(8,128)(2,1)S(1)} fusion(f32[16,80,640]{2,1,0:T(8,128)} %fusion.5, f32[16,80]{1,0:T(8,128)S(1)} %copy.64, f32[16,80]{1,0:T(8,128)S(1)} %dynamic-slice_bitcast_fusion, pred[80,640]{1,0:T(8,128)(4,1)S(1)} %iota_compare_fusion, bf16[80,16,128]{2,1,0:T(8,128)(2,1)S(1)} %bitcast.145, ...), kind=kOutput, calls=%fused_computation | convolution fusion | flops 215449600 | bytes 7925760 | tf_op jit(solution)/shard_map/cond/branch_1_fun/thd,uhd->htu/dot_general | solution.py:45
  109.0 0.7 fusion.18
  109.8 3.2 fusion.23
  113.0 3.4 fusion.12
  116.4 2.7 fusion.79
  119.1 2.7 fusion.74
  121.9 18.9 %conditional.4 = (f32[80,2048]{1,0:T(8,128)S(1)}, f32[640,2048]{0,1:T(8,128)}, f32[640,2048]{0,1:T(8,128)}, bf16[80,2048]{1,0:T(8,128)(2,1)S(1)}) conditional(s32[]{:T(128)} %convert_element_type.108, () %tuple.45, (s32[]{:T(128)}, bf16[1,160,2048]{2,1,0:T(8,128)(2,1)S(1)}, bf16[640,2048]{1,0:T(8,128)(2,1)}, s32[]{:T(128)}, f32[1,16,640]{2,1,0:T(8,128)}, ...), branch_computations={%region_4.5_spmd, %region_5.6_spmd} | conditional | flops 1057802304 | bytes 62449412 | solution.py:139
  121.9 0.8 dynamic-slice_bitcast_fusion.1
  122.8 4.7 %fusion.33 = f32[16,80,640]{2,1,0:T(8,128)} fusion(bf16[80,16,128]{2,1,0:T(8,128)(2,1)S(1)} %bitcast.139, bf16[640,2048]{1,0:T(8,128)(2,1)} %get-tuple-element.129), kind=kOutput, calls=%fused_computation.37 | convolution fusion | flops 209715200 | bytes 6225920 | tf_op jit(solution)/shard_map/cond/branch_1_fun/thd,uhd->htu/dot_general | solution.py:40
  127.7 5.7 %multiply_convert_fusion.1 = bf16[16,80,640]{2,1,0:T(8,128)(2,1)S(1)} fusion(f32[16,80,640]{2,1,0:T(8,128)} %fusion.33, f32[16,80]{1,0:T(8,128)S(1)} %copy.65, f32[16,80]{1,0:T(8,128)S(1)} %dynamic-slice_bitcast_fusion.1, pred[80,640]{1,0:T(8,128)(4,1)S(1)} %iota_compare_fusion.1, bf16[80,16,128]{2,1,0:T(8,128)(2,1)S(1)} %bitcast.147, ...), kind=kOutput, calls=%fused_computation.30 | convolution fusion | flops 215449600 | bytes 7925760 | tf_op jit(solution)/shard_map/cond/branch_1_fun/thd,uhd->htu/dot_general | solution.py:45
  133.4 0.7 fusion.46
  134.2 3.2 fusion.51
  137.5 3.3 fusion.40
  140.8 2.7 fusion.76
  143.4 69.5 %conditional.5 = (f32[1,512,2048]{2,1,0:T(8,128)}, f32[1,512,2048]{2,1,0:T(8,128)}) conditional(s32[]{:T(128)} %convert_element_type.113, () %tuple.47, (f32[640,2048]{0,1:T(8,128)}, f32[640,2048]{0,1:T(8,128)}, f32[640,2048]{0,1:T(8,128)}, f32[640,2048]{0,1:T(8,128)}, bf16[640,512]{1,0:T(8,128)(2,1)S(1)}) %tuple.80), branch_computations={%region_6.7_spmd, %region_7.8_spmd} | conditional | flops 5397020672 | bytes 191103056 | solution.py:152
  143.4 6.0 %copy.66 = f32[640,2048]{1,0:T(8,128)} copy(f32[640,2048]{0,1:T(8,128)} %get-tuple-element.185) | data formatting | bytes 10485760 | tf_op jit(solution)/shard_map
  149.4 6.0 %copy.67 = f32[640,2048]{1,0:T(8,128)} copy(f32[640,2048]{0,1:T(8,128)} %get-tuple-element.186) | data formatting | bytes 10485760 | tf_op jit(solution)/shard_map
  155.5 7.9 %add.68 = f32[640,2048]{1,0:T(8,128)} add(f32[640,2048]{1,0:T(8,128)} %copy.66, f32[640,2048]{1,0:T(8,128)} %copy.67) | non-fusion elementwise | flops 1310720 | bytes 15728640 | tf_op jit(solution)/shard_map/cond/branch_1_fun/add | solution.py:145
  163.4 6.0 %copy.68 = f32[640,2048]{1,0:T(8,128)} copy(f32[640,2048]{0,1:T(8,128)} %get-tuple-element.187) | data formatting | bytes 10485760 | tf_op jit(solution)/shard_map
  169.4 6.1 %copy.69 = f32[640,2048]{1,0:T(8,128)} copy(f32[640,2048]{0,1:T(8,128)} %get-tuple-element.188) | data formatting | bytes 10485760 | tf_op jit(solution)/shard_map
  175.5 5.2 %add.69 = f32[640,2048]{1,0:T(8,128)S(1)} add(f32[640,2048]{1,0:T(8,128)} %copy.68, f32[640,2048]{1,0:T(8,128)} %copy.69) | non-fusion elementwise | flops 1310720 | bytes 15728640 | tf_op jit(solution)/shard_map/cond/branch_1_fun/add | solution.py:145
  180.7 2.3 copy-done.7
  183.0 6.0 %fusion.57 = f32[4096,512]{1,0:T(8,128)} fusion(bf16[640,512]{1,0:T(8,128)(2,1)S(1)} %get-tuple-element.139, f32[640,2048]{1,0:T(8,128)S(1)} %add.69, f32[640,2048]{1,0:T(8,128)S(1)} %bitcast.138), kind=kOutput, calls=%fused_computation.64 | convolution fusion | flops 2694840320 | bytes 19529728 | tf_op jit(solution)/shard_map/cond/branch_1_fun/dot_general | solution.py:10
  189.0 8.7 %add_bitcast_fusion = f32[512,4096]{0,1:T(8,128)S(1)} fusion(f32[4096,512]{1,0:T(8,128)} %fusion.57, bf16[640,512]{1,0:T(8,128)(2,1)S(1)} %get-tuple-element.139, f32[640,2048]{1,0:T(8,128)} %copy-done.7, f32[640,2048]{1,0:T(8,128)S(1)} %bitcast.138), kind=kOutput, calls=%fused_computation.63 | convolution fusion | flops 2699558912 | bytes 27918336 | tf_op jit(solution)/shard_map/cond/branch_1_fun/dot_general | solution.py:10
  197.7 4.2 slice_bitcast_fusion.2
  202.0 5.4 %copy.73 = f32[1,512,2048]{2,1,0:T(8,128)} copy(f32[1,512,2048]{1,2,0:T(8,128)} %get-tuple-element.197) | data formatting | bytes 8388608 | tf_op jit(solution)/shard_map/cond | solution.py:152
  207.4 5.5 %copy.75 = f32[1,512,2048]{2,1,0:T(8,128)} copy(f32[1,512,2048]{1,2,0:T(8,128)} %get-tuple-element.196) | data formatting | bytes 8388608 | tf_op jit(solution)/shard_map/cond | solution.py:152
  212.9 5.6 %add_bitcast_fusion.1 = f32[1,512,2048]{2,1,0:T(8,128)S(1)} fusion(f32[512,2048]{1,0:T(8,128)} %fusion.76, f32[512,2048]{1,0:T(8,128)} %fusion.79, f32[512,2048]{1,0:T(8,128)} %fusion.74, f32[80,2048]{1,0:T(8,128)S(1)} %get-tuple-element.153, bf16[80,2048]{1,0:T(8,128)(2,1)S(1)} %get-tuple-element.152, bf16[160,512]{1,0:T(8,128)(2,1)S(1)} %fusion.65), kind=kOutput, calls=%fused_computation.70 | convolution fusion | flops 171409408 | bytes 17842176 | tf_op jit(solution)/shard_map/dot_general | solution.py:10
  218.5 0.3 copy-done.2
  218.7 9.8 %pad_maximum_fusion.1 = f32[4,512,2048]{2,1,0:T(8,128)} fusion(f32[1,512,2048]{2,1,0:T(8,128)S(1)} %copy-done.2, f32[1,512,2048]{2,1,0:T(8,128)} %get-tuple-element.191, f32[1,512,2048]{2,1,0:T(8,128)} %get-tuple-element.190, f32[1,512,2048]{2,1,0:T(8,128)S(1)} %add_bitcast_fusion.1), kind=kLoop, calls=%fused_computation.69 | loop fusion | flops 12582912 | bytes 33554432 | tf_op jit(solution)/shard_map/stack | solution.py:156
  228.6 168.3 %reduce-scatter.3.cloned.1.call-done = f32[4,64,2048]{2,1,0:T(8,128)} async-done(((f32[4,512,2048]{2,1,0:T(8,128)}), f32[4,64,2048]{2,1,0:T(8,128)}) %reduce-scatter.3.cloned.1.call-update) | async-done | bytes 2097168 | tf_op jit(solution)/shard_map/reduce_scatter | solution.py:157
  396.9 36.5 %reduce-scatter.5.cloned.1.call-done = f32[4,16,2048]{2,1,0:T(8,128)} async-done(((f32[4,64,2048]{2,1,0:T(8,128)}), f32[4,16,2048]{2,1,0:T(8,128)}) %reduce-scatter.5.cloned.1.call-update) | async-done | bytes 524304 | tf_op jit(solution)/shard_map/reduce_scatter | solution.py:158
  (47 shorter events, 1.0 us)
Async XLA Ops:
  6.5 25.0 %copy-start = (bf16[1,160,4096]{2,1,0:T(8,128)(2,1)S(1)}, bf16[1,160,4096]{2,1,0:T(8,128)(2,1)}, u32[]{:S(2)}) copy-start(bf16[1,160,4096]{2,1,0:T(8,128)(2,1)} %param.21) | copy-start | bytes 3932164
  6.5 48.4 %all-gather.5.cloned.1.call-start = ((), (), s32[]{:S(2)}) async-start(), calls=%async_computation.4 | async-start | bytes 3276800 | tf_op jit(solution)/shard_map/all_gather | solution.py:113
  7.3 89.1 %all-gather.7.cloned.1.call-start = ((), (), s32[]{:S(2)}) async-start(), calls=%async_computation.5 | async-start | bytes 3276800 | tf_op jit(solution)/shard_map/all_gather | solution.py:114
  8.0 388.8 %reduce-scatter.3.cloned.1.call-start = ((), (), s32[]{:S(2)}) async-start(), calls=%async_computation.2 | async-start | bytes 18874368 | tf_op jit(solution)/shard_map/reduce_scatter | solution.py:157
  10.2 21.3 %copy-start.8 = (bf16[1,160,2048]{2,1,0:T(8,128)(2,1)S(1)}, bf16[1,160,2048]{2,1,0:T(8,128)(2,1)}, u32[]{:S(2)}) copy-start(bf16[1,160,2048]{2,1,0:T(8,128)(2,1)} %param.19) | copy-start | bytes 1966084
  31.5 5.8 %copy-start.9 = (bf16[1,160,2048]{2,1,0:T(8,128)(2,1)S(1)}, bf16[1,160,2048]{2,1,0:T(8,128)(2,1)}, u32[]{:S(2)}) copy-start(bf16[1,160,2048]{2,1,0:T(8,128)(2,1)} %param.20) | copy-start | bytes 1966084
  103.1 5.9 %copy-start.5 = (bf16[640,2048]{1,0:T(8,128)(2,1)S(1)}, bf16[640,2048]{1,0:T(8,128)(2,1)}, u32[]{:S(2)}) copy-start(bf16[640,2048]{1,0:T(8,128)(2,1)} %get-tuple-element.122) | copy-start | bytes 7864324 | tf_op jit(solution)/shard_map/cond
  109.8 3.3 copy-start.4
  119.1 2.8 copy-start.10
  127.7 5.7 %copy-start.6 = (bf16[640,2048]{1,0:T(8,128)(2,1)S(1)}, bf16[640,2048]{1,0:T(8,128)(2,1)}, u32[]{:S(2)}) copy-start(bf16[640,2048]{1,0:T(8,128)(2,1)} %get-tuple-element.129) | copy-start | bytes 7864324 | tf_op jit(solution)/shard_map/cond
  134.2 3.3 copy-start.3
  140.8 2.7 copy-start.11
  169.4 13.6 %slice-start = ((s8[5242880]{0:T(1024)(128)(4,1)}), s8[1048576]{0:T(1024)(128)(4,1)S(1)}, s32[]{:S(2)}) async-start(s8[5242880]{0:T(1024)(128)(4,1)} %bitcast.137), calls=%async_computation.6 | async-start | bytes 2097152 | tf_op jit(solution)/shard_map/cond
  175.5 7.5 %slice-start.1 = ((s8[5242880]{0:T(1024)(128)(4,1)}), s8[4194304]{0:T(1024)(128)(4,1)S(1)}, s32[]{:S(2)}) async-start(s8[5242880]{0:T(1024)(128)(4,1)} %bitcast.137), calls=%async_computation.7 | async-start | bytes 8388608 | tf_op jit(solution)/shard_map/cond
  180.7 2.3 copy-start.7
  212.9 5.8 %copy-start.2 = (f32[1,512,2048]{2,1,0:T(8,128)S(1)}, f32[1,512,2048]{2,1,0:T(8,128)}, u32[]{:S(2)}) copy-start(f32[1,512,2048]{2,1,0:T(8,128)} %convolution_bitcast_fusion) | copy-start | bytes 12582916
  228.5 204.8 %copy-start.1 = (bf16[1,160,4096]{2,1,0:T(8,128)(2,1)S(1)}, bf16[1,160,4096]{2,1,0:T(8,128)(2,1)}, u32[]{:S(2)}) copy-start(bf16[1,160,4096]{2,1,0:T(8,128)(2,1)} %param.21) | copy-start | bytes 3932164
  228.5 204.8 %reduce-scatter.5.cloned.1.call-start = ((), (), s32[]{:S(2)}) async-start(), calls=%async_computation.3 | async-start | bytes 2621440 | tf_op jit(solution)/shard_map/reduce_scatter | solution.py:158
Sparse Core Ops, SparseCore 0:
  9.2 45.7 all-gather.4
  56.8 39.4 all-gather.6
  228.7 168.1 reduce-scatter.2
  399.7 33.6 reduce-scatter.4
where the time goes:
time: 441 us; the launch traced here: 440 us
  waiting for transfers between devices  265 us (60%)
  matrix products  73.2 us (17%)
  local copies, waits for them, and re-layouts  45.1 us (10%)
  other arithmetic  25.2 us (6%)
  blocking collectives  17.7 us (4%)
  between operations  13.2 us (3%)
    reduce_scatter x1, waiting for transfers between devices, on_device(): summed = lax.psum_scatter(stacked, 'dp', scatter_dimension=1, tiled=True)  168 us
    all_gather x1, waiting for transfers between devices, on_device(): piece_values = lax.all_gather(own_values, 'ctx', axis=0, tiled=True)  41.4 us
    reduce_scatter x1, waiting for transfers between devices, on_device(): summed = lax.psum_scatter(summed, 'ctx', scatter_dimension=1, tiled=True)  36.5 us
    dot_general x7, matrix products, contract_rows(): lax.dot_general(left, right, (((0,), (0,)), ((), ())), preferred_element_...  34.2 us
    another operation x6, local copies, waits for them, and re-layouts  24.2 us
    all_gather x1, blocking collectives, on_device(): piece_reduced = lax.all_gather(reduced_in, 'ctx', axis=0, tiled=True)  17.7 us
    all_gather x1, waiting for transfers between devices, on_device(): piece_keys = lax.all_gather(own_keys, 'ctx', axis=0, tiled=True)  17.6 us
    dot_general x2, matrix products, query_grads(): jnp.einsum('thd,uhd->htu', grad3, value3, preferred_element_type=jnp.floa...  11.6 us
  transfers between devices with their start and end apart: 4, of which 4 were waited for; matrix products, arithmetic and copies ran while one was open for 3% of the time, Pallas kernels for 0%

commit v1 on v0

v1 whole, which is shorter than its diff:
```python
import functools
import math

import jax
import jax.numpy as jnp
from jax import lax
from jax.experimental import pallas as pl
from jax.experimental.pallas import tpu as pltpu
from jax.sharding import PartitionSpec as P

BLOCK = 128


def dot(left, right, dims):
    return lax.dot_general(left, right, (dims, ((), ())), preferred_element_type=jnp.float32)


def head_kernel(
    q_ref, k_ref, v_ref, g_ref, o_ref, sums_ref, rin_ref, rgrad_ref, out_ref, rin_t, rgrad_t, acc
):
    tokens, width = q_ref.shape
    scaling = 1.0 / math.sqrt(width)

    @pl.when(pl.program_id(0) == 0)
    def _():
        rin_t[...] = rin_ref[...].T
        rgrad_t[...] = rgrad_ref[...].T

    product = g_ref[...].astype(jnp.float32) * o_ref[...].astype(jnp.float32)
    deltas = jnp.sum(product.T, axis=0, keepdims=True)
    sums = sums_ref[0]
    row = lax.broadcasted_iota(jnp.int32, (BLOCK, BLOCK), 0)
    col = lax.broadcasted_iota(jnp.int32, (BLOCK, BLOCK), 1)
    causal = row <= col
    for start in range(0, tokens, BLOCK):
        keys = k_ref[start : start + BLOCK]
        values = v_ref[start : start + BLOCK]
        queries = q_ref[start:]
        grads = g_ref[start:]
        scores = dot(keys, queries, ((1,), (1,))) * scaling
        prob = jnp.exp(scores - sums[:, start:])
        diagonal = jnp.where(causal, prob[:, :BLOCK], 0.0)
        if start + BLOCK < tokens:
            prob = jnp.concatenate([diagonal, prob[:, BLOCK:]], axis=1)
        else:
            prob = diagonal
        dprob = dot(values, grads, ((1,), (1,)))
        dscore = prob * (dprob - deltas[:, start:]) * scaling
        score_low = dscore.astype(jnp.bfloat16)
        prob_low = prob.astype(jnp.bfloat16)
        dquery = dot(score_low, keys, ((0,), (0,)))
        if start == 0:
            acc[:, :width] = dquery
        else:
            acc[start:, :width] += dquery
        acc[start : start + BLOCK, width : 2 * width] = dot(score_low, queries, ((1,), (0,)))
        acc[start : start + BLOCK, 2 * width :] = dot(prob_low, grads, ((1,), (0,)))
    full = acc[...]
    upper = full.astype(jnp.bfloat16)
    lower = (full - upper.astype(jnp.float32)).astype(jnp.bfloat16)
    joined = dot(rin_t[...], upper, ((1,), (0,))) + dot(rin_t[...], lower, ((1,), (0,)))
    for index in range(3):
        out_ref[index] = joined[:, index * width : (index + 1) * width].astype(out_ref.dtype)
    out_ref[3] = dot(rgrad_t[...], o_ref[...], ((1,), (0,))).astype(out_ref.dtype)


def head_grads(q, k, v, g, o, sums, rin, rgrad):
    tokens, columns = q.shape
    heads = sums.shape[0]
    width = columns // heads
    rank = rin.shape[1]
    rows = pl.BlockSpec((tokens, width), lambda h: (0, h))
    whole = pl.BlockSpec((tokens, rank), lambda h: (0, 0))
    return pl.pallas_call(
        head_kernel,
        grid=(heads,),
        out_shape=jax.ShapeDtypeStruct((4, rank, columns), jnp.bfloat16),
        in_specs=[rows] * 5 + [pl.BlockSpec((1, 1, tokens), lambda h: (h, 0, 0)), whole, whole],
        out_specs=pl.BlockSpec((4, rank, width), lambda h: (0, 0, h)),
        scratch_shapes=[
            pltpu.VMEM((rank, tokens), jnp.bfloat16),
            pltpu.VMEM((rank, tokens), jnp.bfloat16),
            pltpu.VMEM((tokens, 3 * width), jnp.float32),
        ],
        compiler_params=pltpu.CompilerParams(vmem_limit_bytes=48 * 1024 * 1024),
    )(q, k, v, g, o, sums, rin, rgrad)


def on_device(
    dp_size,
    ctx_size,
    layer_input,
    queries,
    key_rows,
    value_rows,
    attn_out,
    out_grad,
    layer_grad,
    logsum,
    projector,
):
    heads = logsum.shape[1] // ctx_size
    reduced_in = jnp.dot(layer_input[0], projector, preferred_element_type=jnp.float32)
    reduced_grad = jnp.dot(layer_grad[0], projector, preferred_element_type=jnp.float32)
    reduced_in = reduced_in.astype(jnp.bfloat16)
    reduced_grad = reduced_grad.astype(jnp.bfloat16)

    def by_heads(rows):
        return lax.all_to_all(rows[0], "ctx", split_axis=1, concat_axis=0, tiled=True)

    q, k, v, g, o = map(by_heads, (queries, key_rows, value_rows, out_grad, attn_out))
    rin = lax.all_gather(reduced_in, "ctx", axis=0, tiled=True)
    rgrad = lax.all_gather(reduced_grad, "ctx", axis=0, tiled=True)
    sums = lax.dynamic_slice_in_dim(logsum[0], lax.axis_index("ctx") * heads, heads, 0)
    partial = head_grads(q, k, v, g, o, sums[:, None], rin, rgrad)
    count, rank, columns = partial.shape
    pieces = partial.reshape(count, dp_size, rank // dp_size, columns)
    pieces = lax.all_to_all(pieces, "dp", split_axis=1, concat_axis=1, tiled=True)
    summed = jnp.sum(pieces.astype(jnp.float32), axis=1)
    return lax.all_to_all(summed, "ctx", split_axis=1, concat_axis=2, tiled=True)


def solution(mesh):
    rows = P("dp", "ctx", None)
    placed = (rows,) * 7 + (P("dp", None, None), P())
    return jax.shard_map(
        functools.partial(on_device, mesh.shape["dp"], mesh.shape["ctx"]),
        mesh=mesh,
        in_specs=placed,
        out_specs=P(None, ("dp", "ctx"), None),
        check_vma=False,
    )
```

time: 441 us -> 168 us (0.38)
  waiting for transfers between devices: 265 us -> 13.8 us
  blocking collectives: 17.7 us -> 89.6 us
  matrix products: 73.2 us -> 6.47 us
  other arithmetic: 25.2 us -> 0.3 us
  local copies, waits for them, and re-layouts: 45.1 us -> 23.3 us
  starting transfers between devices: 0.12 us -> 20.5 us
  between operations: 13.2 us -> 0.12 us
  Pallas kernels: 0 us -> 12.7 us
    reduce_scatter x2 -> x0, waiting for transfers between devices: 205 us -> none  [the longest x1 168 us: on_device(): summed = lax.psum_scatter(stacked, 'dp', scatter_dimension=1, tiled=True)]
    dot_general x17 -> x1, matrix products: 69.7 us -> 3.03 us  [on_device(): jnp.dot(layer_grad[0], projector, preferred_element_type=jnp.float32)]
    all_to_all x0 -> x2, blocking collectives: none -> 64.5 us  [the longest x1 53.7 us: on_device(): lax.all_to_all(pieces, 'dp', split_axis=1, concat_axis=1, tiled=True)]
    all_gather x2 -> x0, waiting for transfers between devices: 58.9 us -> none  [the longest x1 41.4 us: on_device(): piece_values = lax.all_gather(own_values, 'ctx', axis=0, tiled=True)]
    another operation x7 -> x0, local copies, waits for them, and re-layouts: 28.5 us -> none
    all_to_all x0 -> x5, starting transfers between devices: none -> 20.5 us  [by_heads(): lax.all_to_all(rows[0], 'ctx', split_axis=1, concat_axis=0, tiled=True)]
    all_to_all x0 -> x12, local copies, waits for them, and re-layouts: none -> 18.2 us  [the longest x10 17.2 us: by_heads(): lax.all_to_all(rows[0], 'ctx', split_axis=1, concat_axis=0, tiled=True)]
    cond x22 -> x0, local copies, waits for them, and re-layouts: 14.5 us -> none  [the longest x2 10.9 us: on_device(): grad_key, grad_value = lax.cond(offset <= last_position, project, unchanged)]
  transfers between devices with their start and end apart: 4 -> 5, of which waited for: 4 -> 2; matrix products, arithmetic and copies ran while one was open for 3% -> 8% of each run, Pallas kernels for 0% -> 0%
where the time goes in v1:
time: 168 us; the launch traced here: 167 us
  blocking collectives  89.6 us (53%)
  local copies, waits for them, and re-layouts  23.3 us (14%)
  starting transfers between devices  20.5 us (12%)
  waiting for transfers between devices  13.8 us (8%)
  Pallas kernels  12.7 us (8%)
  matrix products  6.47 us (4%)
    all_to_all x1, blocking collectives, on_device(): lax.all_to_all(pieces, 'dp', split_axis=1, concat_axis=1, tiled=True)  53.7 us
    all_to_all x5, starting transfers between devices, by_heads(): lax.all_to_all(rows[0], 'ctx', split_axis=1, concat_axis=0, tiled=True)  20.5 us
    all_to_all x10, local copies, waits for them, and re-layouts, by_heads(): lax.all_to_all(rows[0], 'ctx', split_axis=1, concat_axis=0, tiled=True)  17.2 us
    all_to_all x5, waiting for transfers between devices, by_heads(): lax.all_to_all(rows[0], 'ctx', split_axis=1, concat_axis=0, tiled=True)  13.8 us
    all_gather x1, blocking collectives, on_device(): rgrad = lax.all_gather(reduced_grad, 'ctx', axis=0, tiled=True)  12.8 us
    pallas_call x1, Pallas kernels, head_grads(): pl.pallas_call(head_kernel, grid=(heads,), out_shape=jax.ShapeDtypeStruct...  12.7 us
    all_gather x1, blocking collectives, on_device(): rin = lax.all_gather(reduced_in, 'ctx', axis=0, tiled=True)  12.3 us
    all_to_all x1, blocking collectives, on_device(): lax.all_to_all(summed, 'ctx', split_axis=1, concat_axis=2, tiled=True)  10.8 us
  transfers between devices with their start and end apart: 5, of which 2 were waited for; matrix products, arithmetic and copies ran while one was open for 8% of the time, Pallas kernels for 0%

profile of v1, /device:TPU:0, one launch (start us, length us, event | category | flops | bytes accessed | tf_op | source)
XLA Modules:
  0.0 166.8 jit_solution(3096430203543751711)
XLA Ops:
  0.0 0.0 copy-start
  0.0 0.0 copy-start.3
  0.0 2.2 %all_to_all.86 = bf16[160,4,512]{2,1,0:T(4,128)(2,1)S(1)} reshape(bf16[1,160,2048]{2,1,0:T(8,128)(2,1)} %param.10) | data formatting | bytes 1310720 | tf_op jit(solution)/shard_map/all_to_all | solution.py:109
  2.2 1.0 copy.34
  3.2 5.2 %all-to-all-start = ((bf16[160,4,512]{2,0,1:T(8,128)(2,1)}), bf16[160,4,512]{2,0,1:T(8,128)(2,1)S(1)}, u32[]{:S(2)}, u32[]{:S(2)}) async-start(bf16[160,4,512]{2,0,1:T(8,128)(2,1)} %copy.34), calls=%async_computation | async-start | bytes 1310720 | tf_op jit(solution)/shard_map/all_to_all | solution.py:109
  8.4 0.0 copy-done.3
  8.4 0.5 all_to_all.90
  8.9 1.0 copy.35
  9.8 8.0 %all-to-all-done = bf16[160,4,512]{2,0,1:T(8,128)(2,1)S(1)} async-done(((bf16[160,4,512]{2,0,1:T(8,128)(2,1)}), bf16[160,4,512]{2,0,1:T(8,128)(2,1)S(1)}, u32[]{:S(2)}, u32[]{:S(2)}) %all-to-all-start) | async-done | bytes 655392 | tf_op jit(solution)/shard_map/all_to_all | solution.py:109
  17.8 3.5 %all-to-all-start.1 = ((bf16[160,4,512]{2,0,1:T(8,128)(2,1)}), bf16[160,4,512]{2,0,1:T(8,128)(2,1)S(1)}, u32[]{:S(2)}, u32[]{:S(2)}) async-start(bf16[160,4,512]{2,0,1:T(8,128)(2,1)} %copy.35), calls=%async_computation.1 | async-start | bytes 1310720 | tf_op jit(solution)/shard_map/all_to_all | solution.py:109
  21.3 2.1 %all_to_all.94 = bf16[160,4,512]{2,1,0:T(4,128)(2,1)S(1)} reshape(bf16[1,160,2048]{2,1,0:T(8,128)(2,1)} %param.12) | data formatting | bytes 1310720 | tf_op jit(solution)/shard_map/all_to_all | solution.py:109
  23.4 1.0 copy.36
  24.4 5.8 %all-to-all-done.1 = bf16[160,4,512]{2,0,1:T(8,128)(2,1)S(1)} async-done(((bf16[160,4,512]{2,0,1:T(8,128)(2,1)}), bf16[160,4,512]{2,0,1:T(8,128)(2,1)S(1)}, u32[]{:S(2)}, u32[]{:S(2)}) %all-to-all-start.1) | async-done | bytes 655392 | tf_op jit(solution)/shard_map/all_to_all | solution.py:109
  30.2 3.5 %all-to-all-start.2 = ((bf16[160,4,512]{2,0,1:T(8,128)(2,1)}), bf16[160,4,512]{2,0,1:T(8,128)(2,1)S(1)}, u32[]{:S(2)}, u32[]{:S(2)}) async-start(bf16[160,4,512]{2,0,1:T(8,128)(2,1)} %copy.36), calls=%async_computation.2 | async-start | bytes 1310720 | tf_op jit(solution)/shard_map/all_to_all | solution.py:109
  33.7 0.7 constant_dynamic-slice_fusion
  34.5 2.7 %all_to_all.102 = bf16[160,4,512]{2,1,0:T(4,128)(2,1)} reshape(bf16[1,160,2048]{2,1,0:T(8,128)(2,1)} %param.13) | data formatting | bytes 1310720 | tf_op jit(solution)/shard_map/all_to_all | solution.py:109
  37.2 2.0 %copy.38 = bf16[160,4,512]{2,0,1:T(8,128)(2,1)} copy(bf16[160,4,512]{2,1,0:T(4,128)(2,1)} %all_to_all.102) | data formatting | bytes 1310720 | tf_op jit(solution)/shard_map/all_to_all | solution.py:109
  39.2 2.7 %all_to_all.98 = bf16[160,4,512]{2,1,0:T(4,128)(2,1)} reshape(bf16[1,160,2048]{2,1,0:T(8,128)(2,1)} %param.14) | data formatting | bytes 1310720 | tf_op jit(solution)/shard_map/all_to_all | solution.py:109
  42.0 2.1 %copy.37 = bf16[160,4,512]{2,0,1:T(8,128)(2,1)} copy(bf16[160,4,512]{2,1,0:T(4,128)(2,1)} %all_to_all.98) | data formatting | bytes 1310720 | tf_op jit(solution)/shard_map/all_to_all | solution.py:109
  44.0 0.0 all-to-all-done.2
  44.0 4.2 %all-to-all-start.4 = ((bf16[160,4,512]{2,0,1:T(8,128)(2,1)}), bf16[160,4,512]{2,0,1:T(8,128)(2,1)}, u32[]{:S(2)}, u32[]{:S(2)}) async-start(bf16[160,4,512]{2,0,1:T(8,128)(2,1)} %copy.38), calls=%async_computation.4 | async-start | bytes 1310720 | tf_op jit(solution)/shard_map/all_to_all | solution.py:109
  48.2 0.0 copy-done
  48.2 3.0 %fusion.7 = bf16[160,512]{1,0:T(8,128)(2,1)S(1)} fusion(bf16[4096,512]{1,0:T(8,128)(2,1)} %param.17, bf16[1,160,4096]{2,1,0:T(8,128)(2,1)S(1)} %copy-done), kind=kOutput, calls=%fused_computation.6 | convolution fusion | flops 671170560 | bytes 5668864 | tf_op jit(solution)/shard_map/dot_general | solution.py:104
  51.2 12.8 %all_gather.7.rgrad_ref = bf16[640,512]{1,0:T(8,128)(2,1)} all-gather(bf16[160,512]{1,0:T(8,128)(2,1)S(1)} %fusion.7), channel_id=1, replica_groups=mesh['dp'=8,'ctx'=4] {'ctx'}, dimensions={0}, use_global_device_ids=true | all-gather | bytes 819200 | tf_op jit(solution)/shard_map/all_gather | solution.py:113
  64.0 0.0 all-to-all-done.4
  64.0 4.2 %all-to-all-start.3 = ((bf16[160,4,512]{2,0,1:T(8,128)(2,1)}), bf16[160,4,512]{2,0,1:T(8,128)(2,1)}, u32[]{:S(2)}, u32[]{:S(2)}) async-start(bf16[160,4,512]{2,0,1:T(8,128)(2,1)} %copy.37), calls=%async_computation.3 | async-start | bytes 1310720 | tf_op jit(solution)/shard_map/all_to_all | solution.py:109
  68.2 3.4 %fusion.4 = bf16[160,512]{1,0:T(8,128)(2,1)S(1)} fusion(bf16[4096,512]{1,0:T(8,128)(2,1)} %param.17, bf16[1,160,4096]{2,1,0:T(8,128)(2,1)} %param.9), kind=kOutput, calls=%fused_computation.5 | convolution fusion | flops 671170560 | bytes 5668864 | tf_op jit(solution)/shard_map/dot_general | solution.py:103
  71.6 12.3 %all_gather.6.rin_ref = bf16[640,512]{1,0:T(8,128)(2,1)} all-gather(bf16[160,512]{1,0:T(8,128)(2,1)S(1)} %fusion.4), channel_id=1, replica_groups=mesh['dp'=8,'ctx'=4] {'ctx'}, dimensions={0}, use_global_device_ids=true | all-gather | bytes 819200 | tf_op jit(solution)/shard_map/all_gather | solution.py:112
  83.9 0.0 all-to-all-done.3
  83.9 0.0 copy-start.1
  84.0 1.1 copy-done.1
  85.0 0.0 copy-start.2
  85.0 1.1 copy-done.2
  86.1 12.7 %shard_map.91 = bf16[4,512,512]{2,1,0:T(8,128)(2,1)} custom-call(bf16[640,512]{1,0:T(8,128)(2,1)S(1)} %bitcast.33, bf16[640,512]{1,0:T(8,128)(2,1)S(1)} %bitcast.34, bf16[640,512]{1,0:T(8,128)(2,1)S(1)} %bitcast.35, bf16[640,512]{1,0:T(8,128)(2,1)} %bitcast.7.g_ref, bf16[640,512]{1,0:T(8,128)(2,1)} %bitcast.9.o_ref, ...), custom_call_target="tpu_custom_call" | custom-call | tf_op jit(solution)/shard_map/pallas_call | solution.py:74
  98.8 1.8 %copy.39 = bf16[4,8,64,512]{3,2,0,1:T(8,128)(2,1)S(1)} copy(bf16[4,8,64,512]{3,2,1,0:T(8,128)(2,1)} %bitcast.36) | data formatting | bytes 4194304 | tf_op jit(solution)/shard_map/reshape | solution.py:117
  100.6 53.7 %all_to_all.118 = bf16[4,8,64,512]{3,2,0,1:T(8,128)(2,1)S(1)} all-to-all(bf16[4,8,64,512]{3,2,0,1:T(8,128)(2,1)S(1)} %copy.39), channel_id=1, replica_groups=mesh['dp'=8,'ctx'=4] {'dp'}, dimensions={1} | all-to-all | bytes 4194304 | tf_op jit(solution)/shard_map/all_to_all | solution.py:118
  154.3 0.3 convert_reduce_fusion
  154.6 0.3 copy.40
  155.0 10.8 %all_to_all.119 = f32[4,64,512]{2,0,1:T(4,128)S(1)} all-to-all(f32[4,64,512]{2,0,1:T(4,128)S(1)} %copy.40), channel_id=1, replica_groups=mesh['dp'=8,'ctx'=4] {'ctx'}, dimensions={1} | all-to-all | bytes 1048576 | tf_op jit(solution)/shard_map/all_to_all | solution.py:120
  165.8 0.2 copy.41
  166.0 0.8 copy.43
  (1 shorter events, 0.0 us)
Async XLA Ops:
  0.0 48.2 %copy-start = (bf16[1,160,4096]{2,1,0:T(8,128)(2,1)S(1)}, bf16[1,160,4096]{2,1,0:T(8,128)(2,1)}, u32[]{:S(2)}) copy-start(bf16[1,160,4096]{2,1,0:T(8,128)(2,1)} %param.15) | copy-start | bytes 3932164
  0.0 8.4 %copy-start.3 = (bf16[1,160,2048]{2,1,0:T(8,128)(2,1)S(1)}, bf16[1,160,2048]{2,1,0:T(8,128)(2,1)}, u32[]{:S(2)}) copy-start(bf16[1,160,2048]{2,1,0:T(8,128)(2,1)} %param.11) | copy-start | bytes 1966084
  3.2 14.6 %all-to-all-start = ((bf16[160,4,512]{2,0,1:T(8,128)(2,1)}), bf16[160,4,512]{2,0,1:T(8,128)(2,1)S(1)}, u32[]{:S(2)}, u32[]{:S(2)}) async-start(bf16[160,4,512]{2,0,1:T(8,128)(2,1)} %copy.34), calls=%async_computation | async-start | bytes 1310720 | tf_op jit(solution)/shard_map/all_to_all | solution.py:109
  17.8 12.4 %all-to-all-start.1 = ((bf16[160,4,512]{2,0,1:T(8,128)(2,1)}), bf16[160,4,512]{2,0,1:T(8,128)(2,1)S(1)}, u32[]{:S(2)}, u32[]{:S(2)}) async-start(bf16[160,4,512]{2,0,1:T(8,128)(2,1)} %copy.35), calls=%async_computation.1 | async-start | bytes 1310720 | tf_op jit(solution)/shard_map/all_to_all | solution.py:109
  30.2 13.8 %all-to-all-start.2 = ((bf16[160,4,512]{2,0,1:T(8,128)(2,1)}), bf16[160,4,512]{2,0,1:T(8,128)(2,1)S(1)}, u32[]{:S(2)}, u32[]{:S(2)}) async-start(bf16[160,4,512]{2,0,1:T(8,128)(2,1)} %copy.36), calls=%async_computation.2 | async-start | bytes 1310720 | tf_op jit(solution)/shard_map/all_to_all | solution.py:109
  44.0 20.0 %all-to-all-start.4 = ((bf16[160,4,512]{2,0,1:T(8,128)(2,1)}), bf16[160,4,512]{2,0,1:T(8,128)(2,1)}, u32[]{:S(2)}, u32[]{:S(2)}) async-start(bf16[160,4,512]{2,0,1:T(8,128)(2,1)} %copy.38), calls=%async_computation.4 | async-start | bytes 1310720 | tf_op jit(solution)/shard_map/all_to_all | solution.py:109
  64.0 19.9 %all-to-all-start.3 = ((bf16[160,4,512]{2,0,1:T(8,128)(2,1)}), bf16[160,4,512]{2,0,1:T(8,128)(2,1)}, u32[]{:S(2)}, u32[]{:S(2)}) async-start(bf16[160,4,512]{2,0,1:T(8,128)(2,1)} %copy.37), calls=%async_computation.3 | async-start | bytes 1310720 | tf_op jit(solution)/shard_map/all_to_all | solution.py:109
  83.9 1.1 copy-start.1
  85.0 1.1 copy-start.2

commit v2 on v1

v2 whole, which is shorter than its diff:
```python
import functools
import math

import jax
import jax.numpy as jnp
from jax import lax
from jax.experimental import pallas as pl
from jax.experimental.pallas import tpu as pltpu
from jax.sharding import PartitionSpec as P

BLOCK = 128
DEPTH = 512
MESH = pl.DeviceIdType.MESH


def dot(left, right, dims):
    return lax.dot_general(left, right, (dims, ((), ())), preferred_element_type=jnp.float32)


def head_products(arrays, head, sums, acc):
    q_ref, k_ref, v_ref, g_ref, o_ref = (arrays.at[index, head] for index in range(5))
    tokens, width = q_ref.shape
    scaling = 1.0 / math.sqrt(width)
    product = g_ref[...].astype(jnp.float32) * o_ref[...].astype(jnp.float32)
    deltas = jnp.sum(product.T, axis=0, keepdims=True)
    row = lax.broadcasted_iota(jnp.int32, (BLOCK, BLOCK), 0)
    col = lax.broadcasted_iota(jnp.int32, (BLOCK, BLOCK), 1)
    causal = row <= col
    for start in range(0, tokens, BLOCK):
        keys = k_ref[start : start + BLOCK]
        values = v_ref[start : start + BLOCK]
        queries = q_ref[start:]
        grads = g_ref[start:]
        scores = dot(keys, queries, ((1,), (1,))) * scaling
        prob = jnp.exp(scores - sums[:, start:])
        diagonal = jnp.where(causal, prob[:, :BLOCK], 0.0)
        if start + BLOCK < tokens:
            prob = jnp.concatenate([diagonal, prob[:, BLOCK:]], axis=1)
        else:
            prob = diagonal
        dprob = dot(values, grads, ((1,), (1,)))
        dscore = prob * (dprob - deltas[:, start:]) * scaling
        score_low = dscore.astype(jnp.bfloat16)
        prob_low = prob.astype(jnp.bfloat16)
        dquery = dot(score_low, keys, ((0,), (0,)))
        if start == 0:
            acc[:, :width] = dquery
        else:
            acc[start:, :width] += dquery
        acc[start : start + BLOCK, width : 2 * width] = dot(score_low, queries, ((1,), (0,)))
        acc[start : start + BLOCK, 2 * width :] = dot(prob_low, grads, ((1,), (0,)))


def kernel(
    dp_size,
    ctx_size,
    layer_input,
    q_hbm,
    k_hbm,
    v_hbm,
    o_hbm,
    g_hbm,
    layer_grad,
    sums_ref,
    projector,
    out_ref,
    arrays,
    rows_in,
    proj,
    proj_acc,
    reduced,
    reduced_t,
    acc,
    own,
    pair_out,
    pair_in,
    z_out,
    z_in,
    final_out,
    final_in,
    load_sem,
    local_sem,
    head_send,
    head_recv,
    red_send,
    red_recv,
    pair_send,
    pair_recv,
    z_send,
    z_recv,
    final_send,
    final_recv,
):
    me = lax.axis_index("ctx")
    place = lax.axis_index("dp")
    core = place % 2
    level = place // 2
    levels = dp_size // 2
    partner = place + 1 - 2 * core
    sources = (q_hbm, k_hbm, v_hbm, g_hbm, o_hbm)
    heads = arrays.shape[1]
    rows = q_hbm.shape[0]
    width = arrays.shape[3]
    depth = projector.shape[0]
    piece = own.shape[4]
    slab = final_out.shape[3]
    mine = pl.ds(pl.multiple_of(me * rows, 16), rows)

    def ctx_peer(d):
        return lax.rem(me + d, ctx_size)

    def columns(owner, head):
        return pl.ds(pl.multiple_of((owner * heads + head) * width, width), width)

    def remote(src, dst, send, recv, **where):
        return pltpu.make_async_remote_copy(
            src_ref=src,
            dst_ref=dst,
            send_sem=send,
            recv_sem=recv,
            device_id=where,
            device_id_type=MESH,
        )

    def local_copy(head, index):
        return pltpu.make_async_copy(
            sources[index].at[:, columns(me, head)],
            arrays.at[index, head, mine],
            local_sem.at[head, index],
        )

    def head_copy(head, index, d):
        peer = ctx_peer(d)
        return remote(
            sources[index].at[:, columns(peer, head)],
            arrays.at[index, head, mine],
            head_send.at[head, index, d - 1],
            head_recv.at[head, index, d - 1],
            ctx=peer,
        )

    def reduced_copy(which, d):
        return remote(
            reduced.at[which, mine],
            reduced.at[which, mine],
            red_send.at[which, d - 1],
            red_recv.at[which, d - 1],
            ctx=ctx_peer(d),
        )

    def pair_copy(head):
        return remote(
            pair_out.at[head],
            pair_in.at[head],
            pair_send.at[head],
            pair_recv.at[head],
            dp=partner,
        )

    def z_copy(head, d):
        peer = lax.rem(level + d, levels)
        return remote(
            z_out.at[head, peer],
            z_in.at[head, d - 1],
            z_send.at[head, d - 1],
            z_recv.at[head, d - 1],
            dp=peer * 2 + core,
        )

    def final_copy(head, d):
        peer = ctx_peer(d)
        return remote(
            final_out.at[head, peer],
            final_in.at[head, d - 1],
            final_send.at[head, d - 1],
            final_recv.at[head, d - 1],
            ctx=peer,
        )

    def start_head(head):
        for index in range(5):
            for d in range(1, ctx_size):
                head_copy(head, index, d).start()
        for index in range(5):
            local_copy(head, index).start()

    loads = (
        pltpu.make_async_copy(projector, proj, load_sem.at[0]),
        pltpu.make_async_copy(layer_input, rows_in.at[:rows], load_sem.at[1]),
        pltpu.make_async_copy(layer_grad, rows_in.at[rows:], load_sem.at[2]),
    )
    for load in loads:
        load.start()
    barrier = pltpu.get_barrier_semaphore()
    for d in range(1, ctx_size):
        pl.semaphore_signal(barrier, inc=1, device_id={"ctx": ctx_peer(d)}, device_id_type=MESH)
    pl.semaphore_signal(barrier, inc=1, device_id={"dp": partner}, device_id_type=MESH)
    for d in range(1, levels):
        peer = lax.rem(level + d, levels) * 2 + core
        pl.semaphore_signal(barrier, inc=1, device_id={"dp": peer}, device_id_type=MESH)
    pl.semaphore_wait(barrier, ctx_size + levels - 1)

    start_head(0)
    for load in loads:
        load.wait()
    proj_acc[...] = jnp.zeros_like(proj_acc)

    @pl.loop(0, depth // DEPTH)
    def _(step):
        at = pl.ds(pl.multiple_of(step * DEPTH, DEPTH), DEPTH)
        proj_acc[...] += dot(rows_in[:, at], proj[at], ((1,), (0,)))

    for which in range(2):
        reduced[which, mine] = proj_acc[which * rows : (which + 1) * rows].astype(jnp.bfloat16)
        for d in range(1, ctx_size):
            reduced_copy(which, d).start()

    @pl.loop(1, heads)
    def _(head):
        start_head(head)

    def compute(head):
        for index in range(5):
            local_copy(head, index).wait()
            for d in range(1, ctx_size):
                head_copy(head, index, d).wait_recv()
        sums = sums_ref[pl.ds(me * heads + head, 1), :]
        head_products(arrays, head, sums, acc)

        @pl.when(head == 0)
        def _():
            for which in range(2):
                for d in range(1, ctx_size):
                    reduced_copy(which, d).wait_recv()
                reduced_t[which] = reduced[which].T

        full = acc[...]
        upper = full.astype(jnp.bfloat16)
        lower = (full - upper.astype(jnp.float32)).astype(jnp.bfloat16)
        left = reduced_t[0]
        joined = dot(left, upper, ((1,), (0,))) + dot(left, lower, ((1,), (0,)))
        last = dot(reduced_t[1], arrays[4, head], ((1,), (0,)))
        for part in range(dp_size):
            span = slice(part * piece, (part + 1) * piece)
            for index in range(3):
                own[head, part // 2, part % 2, index] = joined[
                    span, index * width : (index + 1) * width
                ]
            own[head, part // 2, part % 2, 3] = last[span]
        for to in range(levels):
            pair_out[head, to] = own[head, to, 1 - core].astype(pair_out.dtype)
        pair_copy(head).start()

    def add_pair(head):
        pair_copy(head).wait_recv()
        for to in range(levels):
            total = own[head, to, core] + pair_in[head, to].astype(jnp.float32)
            own[head, to, core] = total
            z_out[head, to] = total.astype(z_out.dtype)
        for d in range(1, levels):
            z_copy(head, d).start()

    def add_levels(head):
        total = own[head, level, core]
        for d in range(1, levels):
            z_copy(head, d).wait_recv()
            total += z_in[head, d - 1].astype(jnp.float32)
        for to in range(ctx_size):
            final_out[head, to] = total[:, to * slab : (to + 1) * slab]
        for d in range(1, ctx_size):
            final_copy(head, d).start()

    @pl.loop(0, heads + 2)
    def _(step):
        @pl.when(step < heads)
        def _():
            compute(step)

        @pl.when(jnp.logical_and(step >= 1, step < heads + 1))
        def _():
            add_pair(step - 1)

        @pl.when(step >= 2)
        def _():
            add_levels(step - 2)

    @pl.loop(0, heads)
    def _(head):
        out_ref[:, :, columns(me, head)] = final_out[head, me]
        for d in range(1, ctx_size):
            final_copy(head, d).wait()
            owner = lax.rem(me + ctx_size - d, ctx_size)
            out_ref[:, :, columns(owner, head)] = final_in[head, d - 1]
        pair_copy(head).wait_send()
        for d in range(1, levels):
            z_copy(head, d).wait_send()
        for index in range(5):
            for d in range(1, ctx_size):
                head_copy(head, index, d).wait_send()

    for which in range(2):
        for d in range(1, ctx_size):
            reduced_copy(which, d).wait_send()


def on_device(
    dp_size,
    ctx_size,
    layer_input,
    queries,
    key_rows,
    value_rows,
    attn_out,
    out_grad,
    layer_grad,
    logsum,
    projector,
):
    rows, features = queries.shape[1:]
    all_heads, tokens = logsum.shape[1:]
    heads = all_heads // ctx_size
    width = features // all_heads
    depth, rank = projector.shape
    levels = dp_size // 2
    piece = rank // dp_size
    slab = piece // ctx_size
    low, wide = jnp.bfloat16, jnp.float32
    dma = pltpu.SemaphoreType.DMA
    anywhere = pl.BlockSpec(memory_space=pl.ANY)
    in_vmem = pl.BlockSpec(memory_space=pltpu.VMEM)
    return pl.pallas_call(
        functools.partial(kernel, dp_size, ctx_size),
        out_shape=jax.ShapeDtypeStruct((4, slab, features), wide),
        in_specs=[anywhere] * 7 + [in_vmem, anywhere],
        out_specs=in_vmem,
        scratch_shapes=[
            pltpu.VMEM((5, heads, tokens, width), low),
            pltpu.VMEM((2 * rows, depth), low),
            pltpu.VMEM((depth, rank), low),
            pltpu.VMEM((2 * rows, rank), wide),
            pltpu.VMEM((2, tokens, rank), low),
            pltpu.VMEM((2, rank, tokens), low),
            pltpu.VMEM((tokens, 3 * width), wide),
            pltpu.VMEM((heads, levels, 2, 4, piece, width), wide),
            pltpu.VMEM((heads, levels, 4, piece, width), low),
            pltpu.VMEM((heads, levels, 4, piece, width), low),
            pltpu.VMEM((heads, levels, 4, piece, width), low),
            pltpu.VMEM((heads, levels - 1, 4, piece, width), low),
            pltpu.VMEM((heads, ctx_size, 4, slab, width), wide),
            pltpu.VMEM((heads, ctx_size - 1, 4, slab, width), wide),
            dma((3,)),
            dma((heads, 5)),
            dma((heads, 5, ctx_size - 1)),
            dma((heads, 5, ctx_size - 1)),
            dma((2, ctx_size - 1)),
            dma((2, ctx_size - 1)),
            dma((heads,)),
            dma((heads,)),
            dma((heads, levels - 1)),
            dma((heads, levels - 1)),
            dma((heads, ctx_size - 1)),
            dma((heads, ctx_size - 1)),
        ],
        compiler_params=pltpu.CompilerParams(
            collective_id=0, has_side_effects=True, vmem_limit_bytes=56 * 1024 * 1024
        ),
    )(
        layer_input[0],
        queries[0],
        key_rows[0],
        value_rows[0],
        attn_out[0],
        out_grad[0],
        layer_grad[0],
        logsum[0],
        projector,
    )


def solution(mesh):
    rows = P("dp", "ctx", None)
    placed = (rows,) * 7 + (P("dp", None, None), P())
    return jax.shard_map(
        functools.partial(on_device, mesh.shape["dp"], mesh.shape["ctx"]),
        mesh=mesh,
        in_specs=placed,
        out_specs=P(None, ("dp", "ctx"), None),
        check_vma=False,
    )
```

time: 168 us -> 80 us (0.48)
  blocking collectives: 89.6 us -> 0 us
  Pallas kernels: 12.7 us -> 77.9 us
  local copies, waits for them, and re-layouts: 23.3 us -> 1.87 us
  starting transfers between devices: 20.5 us -> 0 us
  waiting for transfers between devices: 13.8 us -> 0 us
  matrix products: 6.47 us -> 0 us
    pallas_call x1, Pallas kernels: 12.7 us -> 77.9 us  [on_device(): pl.pallas_call(functools.partial(kernel, dp_size, ctx_size), out_shape=ja...]
    all_to_all x2 -> x0, blocking collectives: 64.5 us -> none  [the longest x1 53.7 us: on_device(): lax.all_to_all(pieces, 'dp', split_axis=1, concat_axis=1, tiled=True)]
    all_gather x2 -> x0, blocking collectives: 25.1 us -> none  [the longest x1 12.8 us: on_device(): rgrad = lax.all_gather(reduced_grad, 'ctx', axis=0, tiled=True)]
    all_to_all x5 -> x0, starting transfers between devices: 20.5 us -> none  [by_heads(): lax.all_to_all(rows[0], 'ctx', split_axis=1, concat_axis=0, tiled=True)]
    all_to_all x12 -> x0, local copies, waits for them, and re-layouts: 18.2 us -> none  [the longest x10 17.2 us: by_heads(): lax.all_to_all(rows[0], 'ctx', split_axis=1, concat_axis=0, tiled=True)]
    all_to_all x5 -> x0, waiting for transfers between devices: 13.8 us -> none  [by_heads(): lax.all_to_all(rows[0], 'ctx', split_axis=1, concat_axis=0, tiled=True)]
    dot_general x2 -> x0, matrix products: 6.47 us -> none  [the longest x1 3.43 us: on_device(): jnp.dot(layer_input[0], projector, preferred_element_type=jnp.float32)]
    reshape x1 -> x0, local copies, waits for them, and re-layouts: 1.81 us -> none  [on_device(): pieces = partial.reshape(count, dp_size, rank // dp_size, columns)]
  transfers between devices with their start and end apart: 5 -> 0, of which waited for: 2 -> 0; matrix products, arithmetic and copies ran while one was open for 8% -> 0% of each run, Pallas kernels for 0% -> 0%
where the time goes in v2:
time: 80 us; the launch traced here: 79.8 us
  Pallas kernels  77.9 us (97%)
  local copies, waits for them, and re-layouts  1.87 us (2%)
    pallas_call x1, Pallas kernels, on_device(): pl.pallas_call(functools.partial(kernel, dp_size, ctx_size), out_shape=ja...  77.9 us
    unnamed x1, local copies, waits for them, and re-layouts  1.87 us

profile of v2, /device:TPU:0, one launch (start us, length us, event | category | flops | bytes accessed | tf_op | source)
XLA Modules:
  0.0 79.8 jit_solution(8403619604269897333)
XLA Ops:
  0.0 77.9 %shard_map.91 = f32[4,16,2048]{2,1,0:T(8,128)} custom-call(bf16[160,4096]{1,0:T(8,128)(2,1)} %bitcast.8, bf16[160,2048]{1,0:T(8,128)(2,1)} %bitcast.10, bf16[160,2048]{1,0:T(8,128)(2,1)} %bitcast.11, bf16[160,2048]{1,0:T(8,128)(2,1)} %bitcast.12, bf16[160,2048]{1,0:T(8,128)(2,1)} %bitcast.13, bf16[160,2048]{1,0:T(8,128)(2,1)} %bitcast.14, ...), custom_call_target="tpu_custom_call" | custom-call | tf_op jit(solution)/shard_map/pallas_call | solution.py:331
  77.9 1.9 %copy.11 = f32[4,16,2048]{2,1,0:T(8,128)} copy(f32[4,16,2048]{2,1,0:T(8,128)} %shard_map.91) | data formatting | bytes 1048576

commit v3 on v2

--- a/solution.py
+++ b/solution.py
@@ -17,12 +17,10 @@
     return lax.dot_general(left, right, (dims, ((), ())), preferred_element_type=jnp.float32)
 
 
-def head_products(arrays, head, sums, acc):
-    q_ref, k_ref, v_ref, g_ref, o_ref = (arrays.at[index, head] for index in range(5))
+def head_products(arrays, head, sums, deltas, acc):
+    q_ref, k_ref, v_ref, g_ref = (arrays.at[index, head] for index in range(4))
     tokens, width = q_ref.shape
     scaling = 1.0 / math.sqrt(width)
-    product = g_ref[...].astype(jnp.float32) * o_ref[...].astype(jnp.float32)
-    deltas = jnp.sum(product.T, axis=0, keepdims=True)
     row = lax.broadcasted_iota(jnp.int32, (BLOCK, BLOCK), 0)
     col = lax.broadcasted_iota(jnp.int32, (BLOCK, BLOCK), 1)
     causal = row <= col
@@ -68,8 +66,14 @@
     rows_in,
     proj,
     proj_acc,
+    grad_own,
+    out_own,
     reduced,
     reduced_t,
+    reduced_grad,
+    delta_out,
+    delta_in,
+    delta_rows,
     acc,
     own,
     pair_out,
@@ -78,18 +82,34 @@
     z_in,
     final_out,
     final_in,
+    own_o,
+    pair_out_o,
+    pair_in_o,
+    z_out_o,
+    z_in_o,
+    final_own_o,
+    final_out_o,
+    final_in_o,
     load_sem,
     local_sem,
     head_send,
     head_recv,
     red_send,
     red_recv,
+    delta_send,
+    delta_recv,
     pair_send,
     pair_recv,
     z_send,
     z_recv,
     final_send,
     final_recv,
+    pair_send_o,
+    pair_recv_o,
+    z_send_o,
+    z_recv_o,
+    final_send_o,
+    final_recv_o,
 ):
     me = lax.axis_index("ctx")
     place = lax.axis_index("dp")
@@ -97,7 +117,8 @@
     level = place // 2
     levels = dp_size // 2
     partner = place + 1 - 2 * core
-    sources = (q_hbm, k_hbm, v_hbm, g_hbm, o_hbm)
+    sources = (q_hbm, k_hbm, v_hbm, g_hbm)
+    count = len(sources)
     heads = arrays.shape[1]
     rows = q_hbm.shape[0]
     width = arrays.shape[3]
@@ -139,13 +160,46 @@
             ctx=peer,
         )
 
-    def reduced_copy(which, d):
-        return remote(
-            reduced.at[which, mine],
-            reduced.at[which, mine],
-            red_send.at[which, d - 1],
-            red_recv.at[which, d - 1],
+    def reduced_copy(d):
+        return remote(
+            reduced.at[mine],
+            reduced.at[mine],
+            red_send.at[d - 1],
+            red_recv.at[d - 1],
             ctx=ctx_peer(d),
+        )
+
+    def delta_copy(d):
+        peer = ctx_peer(d)
+        return remote(
+            delta_out.at[peer],
+            delta_in.at[me],
+            delta_send.at[d - 1],
+            delta_recv.at[d - 1],
+            ctx=peer,
+        )
+
+    def pair_copy_o():
+        return remote(pair_out_o, pair_in_o, pair_send_o, pair_recv_o, dp=partner)
+
+    def z_copy_o(d):
+        peer = lax.rem(level + d, levels)
+        return remote(
+            z_out_o.at[peer],
+            z_in_o.at[d - 1],
+            z_send_o.at[d - 1],
+            z_recv_o.at[d - 1],
+            dp=peer * 2 + core,
+        )
+
+    def final_copy_o(d):
+        peer = ctx_peer(d)
+        return remote(
+            final_out_o.at[peer],
+            final_in_o.at[d - 1],
+            final_send_o.at[d - 1],
+            final_recv_o.at[d - 1],
+            ctx=peer,
         )
 
     def pair_copy(head):
@@ -178,16 +232,18 @@
         )
 
     def start_head(head):
-        for index in range(5):
+        for index in range(count):
             for d in range(1, ctx_size):
                 head_copy(head, index, d).start()
-        for index in range(5):
+        for index in range(count):
             local_copy(head, index).start()
 
     loads = (
         pltpu.make_async_copy(projector, proj, load_sem.at[0]),
         pltpu.make_async_copy(layer_input, rows_in.at[:rows], load_sem.at[1]),
         pltpu.make_async_copy(layer_grad, rows_in.at[rows:], load_sem.at[2]),
+        pltpu.make_async_copy(g_hbm, grad_own, load_sem.at[3]),
+        pltpu.make_async_copy(o_hbm, out_own, load_sem.at[4]),
     )
     for load in loads:
         load.start()
@@ -210,43 +266,85 @@
         at = pl.ds(pl.multiple_of(step * DEPTH, DEPTH), DEPTH)
         proj_acc[...] += dot(rows_in[:, at], proj[at], ((1,), (0,)))
 
-    for which in range(2):
-        reduced[which, mine] = proj_acc[which * rows : (which + 1) * rows].astype(jnp.bfloat16)
-        for d in range(1, ctx_size):
-            reduced_copy(which, d).start()
+    reduced[mine] = proj_acc[:rows].astype(jnp.bfloat16)
+    for d in range(1, ctx_size):
+        reduced_copy(d).start()
+    reduced_grad[...] = proj_acc[rows:].astype(jnp.bfloat16)
+    lane = lax.broadcasted_iota(jnp.int32, (rows, BLOCK), 1)
+    table = jnp.zeros((rows, BLOCK), jnp.float32)
+    for head in range(heads * ctx_size):
+        span = slice(head * width, (head + 1) * width)
+        product = grad_own[:, span].astype(jnp.float32) * out_own[:, span].astype(jnp.float32)
+        table = jnp.where(lane == head, jnp.sum(product, axis=1, keepdims=True), table)
+    table = table.T
+    delta_out[...] = jnp.zeros_like(delta_out)
+    for owner in range(ctx_size):
+        delta_out[owner, :heads] = table[owner * heads : (owner + 1) * heads]
+    delta_in[me] = delta_out[me]
+    for d in range(1, ctx_size):
+        delta_copy(d).start()
 
     @pl.loop(1, heads)
     def _(head):
         start_head(head)
 
+    rgrad_t = reduced_grad[...].T
+    for part in range(dp_size):
+        span = slice(part * piece, (part + 1) * piece)
+        own_o[part // 2, part % 2] = dot(rgrad_t[span], out_own[...], ((1,), (0,)))
+    for to in range(levels):
+        pair_out_o[to] = own_o[to, 1 - core].astype(pair_out_o.dtype)
+    pair_copy_o().start()
+
+    for d in range(1, ctx_size):
+        delta_copy(d).wait_recv()
+    delta_rows[...] = jnp.concatenate([delta_in[owner] for owner in range(ctx_size)], axis=1)
+
+    pair_copy_o().wait_recv()
+    for to in range(levels):
+        total_o = own_o[to, core] + pair_in_o[to].astype(jnp.float32)
+        own_o[to, core] = total_o
+        z_out_o[to] = total_o.astype(z_out_o.dtype)
+    for d in range(1, levels):
+        z_copy_o(d).start()
+
+    def add_levels_o():
+        total = own_o[level, core]
+        for d in range(1, levels):
+            z_copy_o(d).wait_recv()
+            total += z_in_o[d - 1].astype(jnp.float32)
+        for to in range(ctx_size):
+            part = total[to * slab : (to + 1) * slab]
+            final_own_o[to] = part
+            final_out_o[to] = part.astype(final_out_o.dtype)
+        for d in range(1, ctx_size):
+            final_copy_o(d).start()
+
     def compute(head):
-        for index in range(5):
+        for index in range(count):
             local_copy(head, index).wait()
             for d in range(1, ctx_size):
                 head_copy(head, index, d).wait_recv()
         sums = sums_ref[pl.ds(me * heads + head, 1), :]
-        head_products(arrays, head, sums, acc)
+        head_products(arrays, head, sums, delta_rows[pl.ds(head, 1), :], acc)
 
         @pl.when(head == 0)
         def _():
-            for which in range(2):
-                for d in range(1, ctx_size):
-                    reduced_copy(which, d).wait_recv()
-                reduced_t[which] = reduced[which].T
+            for d in range(1, ctx_size):
+                reduced_copy(d).wait_recv()
+            reduced_t[...] = reduced[...].T
 
         full = acc[...]
         upper = full.astype(jnp.bfloat16)
         lower = (full - upper.astype(jnp.float32)).astype(jnp.bfloat16)
-        left = reduced_t[0]
+        left = reduced_t[...]
         joined = dot(left, upper, ((1,), (0,))) + dot(left, lower, ((1,), (0,)))
-        last = dot(reduced_t[1], arrays[4, head], ((1,), (0,)))
         for part in range(dp_size):
             span = slice(part * piece, (part + 1) * piece)
             for index in range(3):
                 own[head, part // 2, part % 2, index] = joined[
                     span, index * width : (index + 1) * width
                 ]
-            own[head, part // 2, part % 2, 3] = last[span]
         for to in range(levels):
             pair_out[head, to] = own[head, to, 1 - core].astype(pair_out.dtype)
         pair_copy(head).start()
@@ -272,6 +370,10 @@
 
     @pl.loop(0, heads + 2)
     def _(step):
+        @pl.when(step == heads - 1)
+        def _():
+            add_levels_o()
+
         @pl.when(step < heads)
         def _():
             compute(step)
@@ -286,21 +388,28 @@
 
     @pl.loop(0, heads)
     def _(head):
-        out_ref[:, :, columns(me, head)] = final_out[head, me]
+        out_ref[:3, :, columns(me, head)] = final_out[head, me]
         for d in range(1, ctx_size):
             final_copy(head, d).wait()
             owner = lax.rem(me + ctx_size - d, ctx_size)
-            out_ref[:, :, columns(owner, head)] = final_in[head, d - 1]
+            out_ref[:3, :, columns(owner, head)] = final_in[head, d - 1]
         pair_copy(head).wait_send()
         for d in range(1, levels):
             z_copy(head, d).wait_send()
-        for index in range(5):
+        for index in range(count):
             for d in range(1, ctx_size):
                 head_copy(head, index, d).wait_send()
 
-    for which in range(2):
-        for d in range(1, ctx_size):
-            reduced_copy(which, d).wait_send()
+    total = final_own_o[me]
+    for d in range(1, ctx_size):
+        reduced_copy(d).wait_send()
+        delta_copy(d).wait_send()
+        final_copy_o(d).wait()
+        total += final_in_o[d - 1].astype(jnp.float32)
+    out_ref[3] = total
+    pair_copy_o().wait_send()
+    for d in range(1, levels):
+        z_copy_o(d).wait_send()
 
 
 def on_device(
@@ -324,6 +433,7 @@
     levels = dp_size // 2
     piece = rank // dp_size
     slab = piece // ctx_size
+    padded = -(-heads // 8) * 8
     low, wide = jnp.bfloat16, jnp.float32
     dma = pltpu.SemaphoreType.DMA
     anywhere = pl.BlockSpec(memory_space=pl.ANY)
@@ -334,32 +444,54 @@
         in_specs=[anywhere] * 7 + [in_vmem, anywhere],
         out_specs=in_vmem,
         scratch_shapes=[
-            pltpu.VMEM((5, heads, tokens, width), low),
+            pltpu.VMEM((4, heads, tokens, width), low),
             pltpu.VMEM((2 * rows, depth), low),
             pltpu.VMEM((depth, rank), low),
             pltpu.VMEM((2 * rows, rank), wide),
-            pltpu.VMEM((2, tokens, rank), low),
-            pltpu.VMEM((2, rank, tokens), low),
+            pltpu.VMEM((rows, features), low),
+            pltpu.VMEM((rows, features), low),
+            pltpu.VMEM((tokens, rank), low),
+            pltpu.VMEM((rank, tokens), low),
+            pltpu.VMEM((rows, rank), low),
+            pltpu.VMEM((ctx_size, padded, rows), wide),
+            pltpu.VMEM((ctx_size, padded, rows), wide),
+            pltpu.VMEM((padded, tokens), wide),
             pltpu.VMEM((tokens, 3 * width), wide),
-            pltpu.VMEM((heads, levels, 2, 4, piece, width), wide),
-            pltpu.VMEM((heads, levels, 4, piece, width), low),
-            pltpu.VMEM((heads, levels, 4, piece, width), low),
-            pltpu.VMEM((heads, levels, 4, piece, width), low),
-            pltpu.VMEM((heads, levels - 1, 4, piece, width), low),
-            pltpu.VMEM((heads, ctx_size, 4, slab, width), wide),
-            pltpu.VMEM((heads, ctx_size - 1, 4, slab, width), wide),
-            dma((3,)),
-            dma((heads, 5)),
-            dma((heads, 5, ctx_size - 1)),
-            dma((heads, 5, ctx_size - 1)),
-            dma((2, ctx_size - 1)),
-            dma((2, ctx_size - 1)),
+            pltpu.VMEM((heads, levels, 2, 3, piece, width), wide),
+            pltpu.VMEM((heads, levels, 3, piece, width), low),
+            pltpu.VMEM((heads, levels, 3, piece, width), low),
+            pltpu.VMEM((heads, levels, 3, piece, width), low),
+            pltpu.VMEM((heads, levels - 1, 3, piece, width), low),
+            pltpu.VMEM((heads, ctx_size, 3, slab, width), wide),
+            pltpu.VMEM((heads, ctx_size - 1, 3, slab, width), wide),
+            pltpu.VMEM((levels, 2, piece, features), wide),
+            pltpu.VMEM((levels, piece, features), low),
+            pltpu.VMEM((levels, piece, features), low),
+            pltpu.VMEM((levels, piece, features), low),
+            pltpu.VMEM((levels - 1, piece, features), low),
+            pltpu.VMEM((ctx_size, slab, features), wide),
+            pltpu.VMEM((ctx_size, slab, features), low),
+            pltpu.VMEM((ctx_size - 1, slab, features), low),
+            dma((5,)),
+            dma((heads, 4)),
+            dma((heads, 4, ctx_size - 1)),
+            dma((heads, 4, ctx_size - 1)),
+            dma((ctx_size - 1,)),
+            dma((ctx_size - 1,)),
+            dma((ctx_size - 1,)),
+            dma((ctx_size - 1,)),
             dma((heads,)),
             dma((heads,)),
             dma((heads, levels - 1)),
             dma((heads, levels - 1)),
             dma((heads, ctx_size - 1)),
             dma((heads, ctx_size - 1)),
+            dma(()),
+            dma(()),
+            dma((levels - 1,)),
+            dma((levels - 1,)),
+            dma((ctx_size - 1,)),
+            dma((ctx_size - 1,)),
         ],
         compiler_params=pltpu.CompilerParams(
             collective_id=0, has_side_effects=True, vmem_limit_bytes=56 * 1024 * 1024

time: 80 us -> 71.9 us (0.90)
  Pallas kernels: 77.9 us -> 69.8 us
    pallas_call x1, Pallas kernels: 77.9 us -> 69.8 us  [on_device(): pl.pallas_call(functools.partial(kernel, dp_size, ctx_size), out_shape=ja...]
where the time goes in v3:
time: 71.9 us; the launch traced here: 71.7 us
  Pallas kernels  69.8 us (97%)
  local copies, waits for them, and re-layouts  1.87 us (3%)
    pallas_call x1, Pallas kernels, on_device(): pl.pallas_call(functools.partial(kernel, dp_size, ctx_size), out_shape=ja...  69.8 us
    unnamed x1, local copies, waits for them, and re-layouts  1.87 us

profile of v3, /device:TPU:0, one launch (start us, length us, event | category | flops | bytes accessed | tf_op | source)
XLA Modules:
  0.0 71.7 jit_solution(9136042241492874962)
XLA Ops:
  0.0 69.8 %shard_map.91 = f32[4,16,2048]{2,1,0:T(8,128)} custom-call(bf16[160,4096]{1,0:T(8,128)(2,1)} %bitcast.8, bf16[160,2048]{1,0:T(8,128)(2,1)} %bitcast.10, bf16[160,2048]{1,0:T(8,128)(2,1)} %bitcast.11, bf16[160,2048]{1,0:T(8,128)(2,1)} %bitcast.12, bf16[160,2048]{1,0:T(8,128)(2,1)} %bitcast.13, bf16[160,2048]{1,0:T(8,128)(2,1)} %bitcast.14, ...), custom_call_target="tpu_custom_call" | custom-call | tf_op jit(solution)/shard_map/pallas_call | solution.py:441
  69.8 1.9 %copy.11 = f32[4,16,2048]{2,1,0:T(8,128)} copy(f32[4,16,2048]{2,1,0:T(8,128)} %shard_map.91) | data formatting | bytes 1048576

commit v4 on v3

--- a/solution.py
+++ b/solution.py
@@ -76,17 +76,13 @@
     delta_rows,
     acc,
     own,
-    pair_out,
-    pair_in,
-    z_out,
-    z_in,
+    sum_out,
+    sum_in,
     final_out,
     final_in,
     own_o,
-    pair_out_o,
-    pair_in_o,
-    z_out_o,
-    z_in_o,
+    sum_out_o,
+    sum_in_o,
     final_own_o,
     final_out_o,
     final_in_o,
@@ -98,32 +94,25 @@
     red_recv,
     delta_send,
     delta_recv,
-    pair_send,
-    pair_recv,
-    z_send,
-    z_recv,
+    sum_send,
+    sum_recv,
     final_send,
     final_recv,
-    pair_send_o,
-    pair_recv_o,
-    z_send_o,
-    z_recv_o,
+    sum_send_o,
+    sum_recv_o,
     final_send_o,
     final_recv_o,
 ):
     me = lax.axis_index("ctx")
     place = lax.axis_index("dp")
-    core = place % 2
-    level = place // 2
-    levels = dp_size // 2
-    partner = place + 1 - 2 * core
+    bits = dp_size.bit_length() - 1
     sources = (q_hbm, k_hbm, v_hbm, g_hbm)
     count = len(sources)
     heads = arrays.shape[1]
     rows = q_hbm.shape[0]
     width = arrays.shape[3]
     depth = projector.shape[0]
-    piece = own.shape[4]
+    piece = own.shape[3]
     slab = final_out.shape[3]
     mine = pl.ds(pl.multiple_of(me * rows, 16), rows)
 
@@ -179,18 +168,42 @@
             ctx=peer,
         )
 
-    def pair_copy_o():
-        return remote(pair_out_o, pair_in_o, pair_send_o, pair_recv_o, dp=partner)
-
-    def z_copy_o(d):
-        peer = lax.rem(level + d, levels)
-        return remote(
-            z_out_o.at[peer],
-            z_in_o.at[d - 1],
-            z_send_o.at[d - 1],
-            z_recv_o.at[d - 1],
-            dp=peer * 2 + core,
-        )
+    group_o = (own_o, sum_out_o, sum_in_o, sum_send_o, sum_recv_o)
+
+    def group_of(head):
+        return tuple(ref.at[head] for ref in (own, sum_out, sum_in, sum_send, sum_recv))
+
+    def place_bit(stage):
+        return lax.rem(place // 2**stage, 2)
+
+    def stage_partner(stage):
+        return place + (1 - 2 * place_bit(stage)) * 2**stage
+
+    def stage_copy(group, stage):
+        half = dp_size // 2 ** (stage + 1)
+        span = pl.ds(dp_size - 2 * half, half)
+        return remote(
+            group[1].at[span],
+            group[2].at[span],
+            group[3].at[stage],
+            group[4].at[stage],
+            dp=stage_partner(stage),
+        )
+
+    def stage_blocks(stage, bit):
+        half = dp_size // 2 ** (stage + 1)
+        first = lax.rem(place, 2**stage) + bit * 2**stage
+        return [(first + 2 ** (stage + 1) * j, dp_size - 2 * half + j) for j in range(half)]
+
+    def send_stage(group, stage):
+        for block, slot in stage_blocks(stage, 1 - place_bit(stage)):
+            group[1][slot] = group[0][block].astype(jnp.bfloat16)
+        stage_copy(group, stage).start()
+
+    def add_stage(group, stage):
+        stage_copy(group, stage).wait_recv()
+        for block, slot in stage_blocks(stage, place_bit(stage)):
+            group[0][block] += group[2][slot].astype(jnp.float32)
 
     def final_copy_o(d):
         peer = ctx_peer(d)
@@ -200,25 +213,6 @@
             final_send_o.at[d - 1],
             final_recv_o.at[d - 1],
             ctx=peer,
-        )
-
-    def pair_copy(head):
-        return remote(
-            pair_out.at[head],
-            pair_in.at[head],
-            pair_send.at[head],
-            pair_recv.at[head],
-            dp=partner,
-        )
-
-    def z_copy(head, d):
-        peer = lax.rem(level + d, levels)
-        return remote(
-            z_out.at[head, peer],
-            z_in.at[head, d - 1],
-            z_send.at[head, d - 1],
-            z_recv.at[head, d - 1],
-            dp=peer * 2 + core,
         )
 
     def final_copy(head, d):
@@ -239,37 +233,25 @@
             local_copy(head, index).start()
 
     loads = (
-        pltpu.make_async_copy(projector, proj, load_sem.at[0]),
-        pltpu.make_async_copy(layer_input, rows_in.at[:rows], load_sem.at[1]),
-        pltpu.make_async_copy(layer_grad, rows_in.at[rows:], load_sem.at[2]),
-        pltpu.make_async_copy(g_hbm, grad_own, load_sem.at[3]),
-        pltpu.make_async_copy(o_hbm, out_own, load_sem.at[4]),
+        pltpu.make_async_copy(g_hbm, grad_own, load_sem.at[0]),
+        pltpu.make_async_copy(o_hbm, out_own, load_sem.at[1]),
+        pltpu.make_async_copy(projector, proj, load_sem.at[2]),
+        pltpu.make_async_copy(layer_input, rows_in.at[:rows], load_sem.at[3]),
+        pltpu.make_async_copy(layer_grad, rows_in.at[rows:], load_sem.at[4]),
     )
     for load in loads:
         load.start()
     barrier = pltpu.get_barrier_semaphore()
     for d in range(1, ctx_size):
         pl.semaphore_signal(barrier, inc=1, device_id={"ctx": ctx_peer(d)}, device_id_type=MESH)
-    pl.semaphore_signal(barrier, inc=1, device_id={"dp": partner}, device_id_type=MESH)
-    for d in range(1, levels):
-        peer = lax.rem(level + d, levels) * 2 + core
+    for stage in range(bits):
+        peer = stage_partner(stage)
         pl.semaphore_signal(barrier, inc=1, device_id={"dp": peer}, device_id_type=MESH)
-    pl.semaphore_wait(barrier, ctx_size + levels - 1)
+    pl.semaphore_wait(barrier, ctx_size - 1 + bits)
 
     start_head(0)
-    for load in loads:
+    for load in loads[:2]:
         load.wait()
-    proj_acc[...] = jnp.zeros_like(proj_acc)
-
-    @pl.loop(0, depth // DEPTH)
-    def _(step):
-        at = pl.ds(pl.multiple_of(step * DEPTH, DEPTH), DEPTH)
-        proj_acc[...] += dot(rows_in[:, at], proj[at], ((1,), (0,)))
-
-    reduced[mine] = proj_acc[:rows].astype(jnp.bfloat16)
-    for d in range(1, ctx_size):
-        reduced_copy(d).start()
-    reduced_grad[...] = proj_acc[rows:].astype(jnp.bfloat16)
     lane = lax.broadcasted_iota(jnp.int32, (rows, BLOCK), 1)
     table = jnp.zeros((rows, BLOCK), jnp.float32)
     for head in range(heads * ctx_size):
@@ -284,6 +266,20 @@
     for d in range(1, ctx_size):
         delta_copy(d).start()
 
+    for load in loads[2:]:
+        load.wait()
+    proj_acc[...] = jnp.zeros_like(proj_acc)
+
+    @pl.loop(0, depth // DEPTH)
+    def _(step):
+        at = pl.ds(pl.multiple_of(step * DEPTH, DEPTH), DEPTH)
+        proj_acc[...] += dot(rows_in[:, at], proj[at], ((1,), (0,)))
+
+    reduced[mine] = proj_acc[:rows].astype(jnp.bfloat16)
+    for d in range(1, ctx_size):
+        reduced_copy(d).start()
+    reduced_grad[...] = proj_acc[rows:].astype(jnp.bfloat16)
+
     @pl.loop(1, heads)
     def _(head):
         start_head(head)
@@ -291,28 +287,22 @@
     rgrad_t = reduced_grad[...].T
     for part in range(dp_size):
         span = slice(part * piece, (part + 1) * piece)
-        own_o[part // 2, part % 2] = dot(rgrad_t[span], out_own[...], ((1,), (0,)))
-    for to in range(levels):
-        pair_out_o[to] = own_o[to, 1 - core].astype(pair_out_o.dtype)
-    pair_copy_o().start()
+        own_o[part] = dot(rgrad_t[span], out_own[...], ((1,), (0,)))
+    send_stage(group_o, 0)
 
     for d in range(1, ctx_size):
         delta_copy(d).wait_recv()
     delta_rows[...] = jnp.concatenate([delta_in[owner] for owner in range(ctx_size)], axis=1)
 
-    pair_copy_o().wait_recv()
-    for to in range(levels):
-        total_o = own_o[to, core] + pair_in_o[to].astype(jnp.float32)
-        own_o[to, core] = total_o
-        z_out_o[to] = total_o.astype(z_out_o.dtype)
-    for d in range(1, levels):
-        z_copy_o(d).start()
-
-    def add_levels_o():
-        total = own_o[level, core]
-        for d in range(1, levels):
-            z_copy_o(d).wait_recv()
-            total += z_in_o[d - 1].astype(jnp.float32)
+    def advance_o(stage):
+        add_stage(group_o, stage)
+        if stage + 1 < bits:
+            send_stage(group_o, stage + 1)
+        else:
+            finish_o()
+
+    def finish_o():
+        total = own_o[place]
         for to in range(ctx_size):
             part = total[to * slab : (to + 1) * slab]
             final_own_o[to] = part
@@ -342,49 +332,43 @@
         for part in range(dp_size):
             span = slice(part * piece, (part + 1) * piece)
             for index in range(3):
-                own[head, part // 2, part % 2, index] = joined[
+                own[head, part, index] = joined[
                     span, index * width : (index + 1) * width
                 ]
-        for to in range(levels):
-            pair_out[head, to] = own[head, to, 1 - core].astype(pair_out.dtype)
-        pair_copy(head).start()
-
-    def add_pair(head):
-        pair_copy(head).wait_recv()
-        for to in range(levels):
-            total = own[head, to, core] + pair_in[head, to].astype(jnp.float32)
-            own[head, to, core] = total
-            z_out[head, to] = total.astype(z_out.dtype)
-        for d in range(1, levels):
-            z_copy(head, d).start()
-
-    def add_levels(head):
-        total = own[head, level, core]
-        for d in range(1, levels):
-            z_copy(head, d).wait_recv()
-            total += z_in[head, d - 1].astype(jnp.float32)
+        send_stage(group_of(head), 0)
+
+    def advance(head, stage):
+        add_stage(group_of(head), stage)
+        if stage + 1 < bits:
+            send_stage(group_of(head), stage + 1)
+        else:
+            finish(head)
+
+    def finish(head):
+        total = own[head, place]
         for to in range(ctx_size):
             final_out[head, to] = total[:, to * slab : (to + 1) * slab]
         for d in range(1, ctx_size):
             final_copy(head, d).start()
 
-    @pl.loop(0, heads + 2)
+    advance_o(0)
+
+    @pl.loop(0, heads + bits - 1)
     def _(step):
-        @pl.when(step == heads - 1)
-        def _():
-            add_levels_o()
-
         @pl.when(step < heads)
         def _():
             compute(step)
-
-        @pl.when(jnp.logical_and(step >= 1, step < heads + 1))
-        def _():
-            add_pair(step - 1)
-
-        @pl.when(step >= 2)
-        def _():
-            add_levels(step - 2)
+            advance(step, 0)
+
+        for stage in range(1, bits):
+
+            @pl.when(step == stage - 1)
+            def _():
+                advance_o(stage)
+
+            @pl.when(jnp.logical_and(step >= stage, step < heads + stage))
+            def _():
+                advance(step - stage, stage)
 
     @pl.loop(0, heads)
     def _(head):
@@ -393,9 +377,8 @@
             final_copy(head, d).wait()
             owner = lax.rem(me + ctx_size - d, ctx_size)
             out_ref[:3, :, columns(owner, head)] = final_in[head, d - 1]
-        pair_copy(head).wait_send()
-        for d in range(1, levels):
-            z_copy(head, d).wait_send()
+        for stage in range(bits):
+            stage_copy(group_of(head), stage).wait_send()
         for index in range(count):
             for d in range(1, ctx_size):
                 head_copy(head, index, d).wait_send()
@@ -407,9 +390,8 @@
         final_copy_o(d).wait()
         total += final_in_o[d - 1].astype(jnp.float32)
     out_ref[3] = total
-    pair_copy_o().wait_send()
-    for d in range(1, levels):
-        z_copy_o(d).wait_send()
+    for stage in range(bits):
+        stage_copy(group_o, stage).wait_send()
 
 
 def on_device(
@@ -430,7 +412,7 @@
     heads = all_heads // ctx_size
     width = features // all_heads
     depth, rank = projector.shape
-    levels = dp_size // 2
+    bits = dp_size.bit_length() - 1
     piece = rank // dp_size
     slab = piece // ctx_size
     padded = -(-heads // 8) * 8
@@ -457,18 +439,14 @@
             pltpu.VMEM((ctx_size, padded, rows), wide),
             pltpu.VMEM((padded, tokens), wide),
             pltpu.VMEM((tokens, 3 * width), wide),
-            pltpu.VMEM((heads, levels, 2, 3, piece, width), wide),
-            pltpu.VMEM((heads, levels, 3, piece, width), low),
-            pltpu.VMEM((heads, levels, 3, piece, width), low),
-            pltpu.VMEM((heads, levels, 3, piece, width), low),
-            pltpu.VMEM((heads, levels - 1, 3, piece, width), low),
+            pltpu.VMEM((heads, dp_size, 3, piece, width), wide),
+            pltpu.VMEM((heads, dp_size - 1, 3, piece, width), low),
+            pltpu.VMEM((heads, dp_size - 1, 3, piece, width), low),
             pltpu.VMEM((heads, ctx_size, 3, slab, width), wide),
             pltpu.VMEM((heads, ctx_size - 1, 3, slab, width), wide),
-            pltpu.VMEM((levels, 2, piece, features), wide),
-            pltpu.VMEM((levels, piece, features), low),
-            pltpu.VMEM((levels, piece, features), low),
-            pltpu.VMEM((levels, piece, features), low),
-            pltpu.VMEM((levels - 1, piece, features), low),
+            pltpu.VMEM((dp_size, piece, features), wide),
+            pltpu.VMEM((dp_size - 1, piece, features), low),
+            pltpu.VMEM((dp_size - 1, piece, features), low),
             pltpu.VMEM((ctx_size, slab, features), wide),
             pltpu.VMEM((ctx_size, slab, features), low),
             pltpu.VMEM((ctx_size - 1, slab, features), low),
@@ -480,16 +458,12 @@
             dma((ctx_size - 1,)),
             dma((ctx_size - 1,)),
             dma((ctx_size - 1,)),
-            dma((heads,)),
-            dma((heads,)),
-            dma((heads, levels - 1)),
-            dma((heads, levels - 1)),
+            dma((heads, bits)),
+            dma((heads, bits)),
             dma((heads, ctx_size - 1)),
             dma((heads, ctx_size - 1)),
-            dma(()),
-            dma(()),
-            dma((levels - 1,)),
-            dma((levels - 1,)),
+            dma((bits,)),
+            dma((bits,)),
             dma((ctx_size - 1,)),
             dma((ctx_size - 1,)),
         ],

time: 71.9 us -> 65.2 us (0.907)
  Pallas kernels: 69.8 us -> 63.1 us
    pallas_call x1, Pallas kernels: 69.8 us -> 63.1 us  [on_device(): pl.pallas_call(functools.partial(kernel, dp_size, ctx_size), out_shape=ja...]
where the time goes in v4:
time: 65.2 us; the launch traced here: 65 us
  Pallas kernels  63.1 us (97%)
  local copies, waits for them, and re-layouts  1.87 us (3%)
    pallas_call x1, Pallas kernels, on_device(): pl.pallas_call(functools.partial(kernel, dp_size, ctx_size), out_shape=ja...  63.1 us
    unnamed x1, local copies, waits for them, and re-layouts  1.87 us

profile of v4, /device:TPU:0, one launch (start us, length us, event | category | flops | bytes accessed | tf_op | source)
XLA Modules:
  0.0 65.0 jit_solution(15183585927251130718)
XLA Ops:
  0.0 63.1 %shard_map.91 = f32[4,16,2048]{2,1,0:T(8,128)} custom-call(bf16[160,4096]{1,0:T(8,128)(2,1)} %bitcast.8, bf16[160,2048]{1,0:T(8,128)(2,1)} %bitcast.10, bf16[160,2048]{1,0:T(8,128)(2,1)} %bitcast.11, bf16[160,2048]{1,0:T(8,128)(2,1)} %bitcast.12, bf16[160,2048]{1,0:T(8,128)(2,1)} %bitcast.13, bf16[160,2048]{1,0:T(8,128)(2,1)} %bitcast.14, ...), custom_call_target="tpu_custom_call" | custom-call | tf_op jit(solution)/shard_map/pallas_call | solution.py:423
  63.1 1.9 %copy.11 = f32[4,16,2048]{2,1,0:T(8,128)} copy(f32[4,16,2048]{2,1,0:T(8,128)} %shard_map.91) | data formatting | bytes 1048576
